TPU v7x, 512 devices: a whole 4x4x16 slice. The times are simulated.
512 devices in a mesh: tensor: 8 (over x, core), wide: 64 (over z, y).
Axes of the slice: x: 4, y: 4, z: 16, core: 2. Of those that a mesh axis runs over, the one named last changes fastest.
Arguments:
- tokens: bfloat16 [512, 3072], P('wide', 'tensor'), may hold values from -6 to 6
- cotangent: bfloat16 [512, 3072], P('wide', 'tensor'), may hold values from -1.5 to 1.5
- gates: bfloat16 [512, 2], P('wide'), may hold values from 0.19921875 to 1
- experts: int32 [512, 2], P('wide'), may hold values from 0 to 7, all different within a row; in each aligned block of 8 rows (0 to 7, 8 to 15, ...) at most 4 rows name the same one
- w_gate: bfloat16 [64, 3072, 1024], P('wide', None, 'tensor'), may hold values from -0.109375 to 0.109375
- w_up: bfloat16 [64, 3072, 1024], P('wide', None, 'tensor'), may hold values from -0.109375 to 0.109375
- w_down: bfloat16 [64, 1024, 3072], P('wide', 'tensor'), may hold values from -0.0625 to 0.0625
Outputs:
- input_grad: bfloat16 [512, 3072], P('wide', 'tensor')
- routing_grad: float32 [512, 2], P('wide')
- gate_proj_grad: bfloat16 [64, 3072, 1024], P('wide', None, 'tensor')
- up_proj_grad: bfloat16 [64, 3072, 1024], P('wide', None, 'tensor')
- down_proj_grad: bfloat16 [64, 1024, 3072], P('wide', 'tensor')
Inputs may be any that keep to these rules, and one draw needn't show every extreme that they name: Each token names 2 different experts. Among the 8 tokens of one index of wide (aligned blocks of rows) no expert is named more than 4 times, and in every draw some expert is named exactly 4 times by some block.
All inputs are finite; a program needn't handle non-finite values.
Results may differ from a plain program's by a relative error of at most 0.02.
Values may be sent and summed in bfloat16 or wider, within the bound.
A program may use at most 64 MiB of HBM per device.

v0:
```python
import jax
import jax.numpy as jnp
from jax import lax
from jax.sharding import PartitionSpec as P

E = 8
CAP = 4


def contract_rows(left_side, right_side):
    return lax.dot_general(
        left_side, right_side, (((0,), (0,)), ((), ())), preferred_element_type=jnp.float32
    )


def contract_cols(left_side, right_side):
    return lax.dot_general(
        left_side, right_side, (((1,), (1,)), ((), ())), preferred_element_type=jnp.float32
    )


def shards(tokens, cotangent, gates, experts, w_gate, w_up, w_down):
    n_wide = lax.axis_size("wide")
    replicas = n_wide // E
    tok_count = tokens.shape[0]
    feature_width = w_gate.shape[1]
    slot_rows = n_wide * CAP
    chosen = experts[:, :, None] == jnp.arange(E, dtype=jnp.int32)[None, None, :]
    picked = jnp.sum(chosen.astype(jnp.int32), axis=1)
    before = jnp.cumsum(picked, axis=0) - picked
    slot_table = (picked[:, :, None] == 1) & (
        before[:, :, None] == jnp.arange(CAP, dtype=jnp.int32)[None, None, :]
    )
    route_matrix = slot_table.reshape(tok_count, E * CAP).astype(jnp.bfloat16)
    gate_each = jnp.sum(jnp.where(chosen, gates[:, :, None].astype(jnp.float32), 0.0), axis=1)
    slot_gate = jnp.sum(jnp.where(slot_table, gate_each[:, :, None], 0.0), axis=0).astype(
        jnp.bfloat16
    )
    gate_sent = jnp.broadcast_to(slot_gate.reshape(E, 1, CAP), (E, replicas, CAP)).reshape(
        n_wide, CAP
    )

    def spread(slot_block):
        columns = slot_block.shape[-1]
        widened = jnp.broadcast_to(
            slot_block.reshape(E, 1, CAP, columns), (E, replicas, CAP, columns)
        )
        return widened.reshape(n_wide, CAP, columns)

    def select(source):
        return contract_rows(route_matrix, source).astype(jnp.bfloat16)

    full_in, full_up = (
        lax.all_gather(tokens, "tensor", axis=1, tiled=True),
        lax.all_gather(cotangent, "tensor", axis=1, tiled=True),
    )
    got_in, got_up, got_gate = (
        lax.all_to_all(spread(select(full_in)), "wide", split_axis=0, concat_axis=0, tiled=True),
        lax.all_to_all(spread(select(full_up)), "wide", split_axis=0, concat_axis=0, tiled=True),
        lax.all_to_all(gate_sent, "wide", split_axis=0, concat_axis=0, tiled=True),
    )
    inputs = got_in.reshape(slot_rows, feature_width)
    upstream = got_up.reshape(slot_rows, feature_width)
    slot_scale = got_gate.reshape(slot_rows).astype(jnp.float32)
    w_first = w_gate[0]
    w_second = w_up[0]
    w_out = w_down[0]
    pre_gate = jnp.dot(inputs, w_first, preferred_element_type=jnp.float32)
    pre_up = jnp.dot(inputs, w_second, preferred_element_type=jnp.float32)
    sigmoid_gate = jax.nn.sigmoid(pre_gate)
    active = pre_gate * sigmoid_gate
    hidden = active * pre_up
    weighted = (slot_scale[:, None] * hidden).astype(jnp.bfloat16)
    through = contract_cols(upstream, w_out)
    gate_terms = lax.psum(jnp.sum(through * hidden, axis=1), "tensor")
    hidden_grad = slot_scale[:, None] * through
    grad_pre_gate = (
        hidden_grad * pre_up * sigmoid_gate * (1.0 + pre_gate * (1.0 - sigmoid_gate))
    ).astype(jnp.bfloat16)
    grad_pre_up = (hidden_grad * active).astype(jnp.bfloat16)
    gate_proj_grad = contract_rows(inputs, grad_pre_gate).astype(jnp.bfloat16)[None]
    up_proj_grad = contract_rows(inputs, grad_pre_up).astype(jnp.bfloat16)[None]
    down_proj_grad = contract_rows(weighted, upstream).astype(jnp.bfloat16)[None]
    returned = contract_cols(grad_pre_gate, w_first) + contract_cols(grad_pre_up, w_second)
    back_rows, back_gate = (
        lax.all_to_all(
            returned.reshape(n_wide, CAP, feature_width).astype(jnp.bfloat16),
            "wide",
            split_axis=0,
            concat_axis=0,
            tiled=True,
        ).astype(jnp.float32),
        lax.all_to_all(
            gate_terms.reshape(n_wide, CAP).astype(jnp.bfloat16),
            "wide",
            split_axis=0,
            concat_axis=0,
            tiled=True,
        ).astype(jnp.float32),
    )
    summed_rows = jnp.sum(back_rows.reshape(E, replicas, CAP, feature_width), axis=1).reshape(
        E * CAP, feature_width
    )
    summed_gate = jnp.sum(back_gate.reshape(E, replicas, CAP), axis=1)
    full_grad = jnp.dot(
        route_matrix.astype(jnp.float32), summed_rows, precision=lax.Precision.HIGHEST
    )
    input_grad = lax.psum_scatter(
        full_grad.astype(jnp.bfloat16), "tensor", scatter_dimension=1, tiled=True
    )
    per_expert = jnp.sum(jnp.where(slot_table, summed_gate[None, :, :], 0.0), axis=2)
    routing_grad = jnp.sum(jnp.where(chosen, per_expert[:, None, :], 0.0), axis=2)
    return (input_grad, routing_grad, gate_proj_grad, up_proj_grad, down_proj_grad)


def solution(mesh):
    return jax.shard_map(
        shards,
        mesh=mesh,
        in_specs=(
            P("wide", "tensor"),
            P("wide", "tensor"),
            P("wide", None),
            P("wide", None),
            P("wide", None, "tensor"),
            P("wide", None, "tensor"),
            P("wide", "tensor", None),
        ),
        out_specs=(
            P("wide", "tensor"),
            P("wide", None),
            P("wide", None, "tensor"),
            P("wide", None, "tensor"),
            P("wide", "tensor", None),
        ),
        check_vma=False,
    )
```

profile of v0, /device:TPU:16, one launch (start us, length us, event | category | flops | bytes accessed | tf_op | source)
XLA Modules:
  0.0 394.5 jit_solution(10497933329953784401)
XLA Ops:
  7.2 0.8 convert_reduce_fusion.2
  8.0 0.1 copy.39
  8.2 0.1 eq.58
  8.3 13.4 %all_gather.7 = bf16[8,3072]{1,0:T(8,128)(2,1)S(1)} all-gather(bf16[8,384]{1,0:T(8,128)(2,1)} %param.7), channel_id=1, replica_groups=mesh['tensor'=8,'wide'=64] {'tensor'}, dimensions={1}, use_global_device_ids=true | all-gather | bytes 55296 | tf_op jit(solution)/shard_map/all_gather | solution.py:54
  21.7 0.1 compare_and_fusion
  21.7 0.2 convolution_convert_fusion.3
  21.9 0.1 broadcast_in_dim.90
  22.0 1.6 broadcast_in_dim.91
  23.7 18.7 %all-to-all-start.2 = ((bf16[64,4,3072]{2,1,0:T(4,128)(2,1)}), bf16[64,4,3072]{2,1,0:T(4,128)(2,1)S(1)}, u32[]{:S(2)}, u32[]{:S(2)}) async-start(bf16[64,4,3072]{2,1,0:T(4,128)(2,1)} %bitcast.54), calls=%async_computation.2 | async-start | bytes 3145728 | tf_op jit(solution)/shard_map/all_to_all | solution.py:58
  42.4 12.8 %all_gather.6 = bf16[8,3072]{1,0:T(8,128)(2,1)S(1)} all-gather(bf16[8,384]{1,0:T(8,128)(2,1)S(1)} %copy-done.6), channel_id=1, replica_groups=mesh['tensor'=8,'wide'=64] {'tensor'}, dimensions={1}, use_global_device_ids=true | all-gather | bytes 55296 | tf_op jit(solution)/shard_map/all_gather | solution.py:55
  55.2 0.2 convolution_convert_fusion.4
  55.4 0.1 broadcast_in_dim.88
  55.5 65.1 %all-to-all-done.2 = bf16[64,4,3072]{2,1,0:T(4,128)(2,1)S(1)} async-done(((bf16[64,4,3072]{2,1,0:T(4,128)(2,1)}), bf16[64,4,3072]{2,1,0:T(4,128)(2,1)S(1)}, u32[]{:S(2)}, u32[]{:S(2)}) %all-to-all-start.2) | async-done | bytes 1572896 | tf_op jit(solution)/shard_map/all_to_all | solution.py:58
  120.6 1.7 broadcast_in_dim.89
  122.2 6.2 %all-to-all-start.1 = ((bf16[64,4,3072]{2,1,0:T(4,128)(2,1)}), bf16[64,4,3072]{2,1,0:T(4,128)(2,1)}, u32[]{:S(2)}, u32[]{:S(2)}) async-start(bf16[64,4,3072]{2,1,0:T(4,128)(2,1)} %bitcast.55), calls=%async_computation.1 | async-start | bytes 3145728 | tf_op jit(solution)/shard_map/all_to_all | solution.py:59
  128.5 2.7 reshape.96
  131.3 0.7 fusion.7
  131.9 0.5 copy-done.3
  132.4 0.7 fusion.10
  133.1 72.8 %all-to-all-done.1 = bf16[64,4,3072]{2,1,0:T(4,128)(2,1)} async-done(((bf16[64,4,3072]{2,1,0:T(4,128)(2,1)}), bf16[64,4,3072]{2,1,0:T(4,128)(2,1)}, u32[]{:S(2)}, u32[]{:S(2)}) %all-to-all-start.1) | async-done | bytes 1572896 | tf_op jit(solution)/shard_map/all_to_all | solution.py:59
  205.8 3.7 reshape.94
  209.5 2.9 multiply_reduce_fusion
  212.5 12.4 %psum.7 = bf16[256]{0:T(256)(128)(2,1)S(1)} all-reduce(f32[256]{0:T(256)S(1)} %get-tuple-element.9), channel_id=1, replica_groups=mesh['tensor'=8,'wide'=64] {'tensor'}, use_global_device_ids=true, to_apply=%region_7.8 | all-reduce | flops 256 | bytes 1536 | tf_op jit(solution)/shard_map/psum | solution.py:75
  224.9 0.7 convert_element_type.106
  225.6 6.9 %all-to-all-start.4 = ((bf16[64,1,4]{2,1,0:T(2,128)(2,1)}), bf16[64,1,4]{2,1,0:T(2,128)(2,1)S(1)}, u32[]{:S(2)}, u32[]{:S(2)}) async-start(bf16[64,1,4]{2,1,0:T(2,128)(2,1)} %convert_element_type.106), calls=%async_computation.4 | async-start | bytes 65536 | tf_op jit(solution)/shard_map/all_to_all | solution.py:93
  232.7 12.7 %all-to-all-done.4 = bf16[64,1,4]{2,1,0:T(2,128)(2,1)S(1)} async-done(((bf16[64,1,4]{2,1,0:T(2,128)(2,1)}), bf16[64,1,4]{2,1,0:T(2,128)(2,1)S(1)}, u32[]{:S(2)}, u32[]{:S(2)}) %all-to-all-start.4) | async-done | bytes 544 | tf_op jit(solution)/shard_map/all_to_all | solution.py:93
  245.4 0.1 select_reduce_fusion
  245.5 0.1 copy.42
  245.7 0.1 all_to_all.19
  245.8 0.1 copy.43
  245.9 18.4 %all_to_all.30 = bf16[64,1,4]{2,1,0:T(2,128)(2,1)S(1)} all-to-all(bf16[64,1,4]{2,1,0:T(2,128)(2,1)S(1)} %copy.43), channel_id=1, replica_groups=mesh['tensor'=8,'wide'=64] {'wide'}, dimensions={0} | all-to-all | bytes 1024 | tf_op jit(solution)/shard_map/all_to_all | solution.py:60
  264.3 0.1 convert_reduce_fusion.1
  264.4 0.1 reshape.99
  264.5 1.0 multiply_convert_fusion.1
  265.5 0.6 fusion.5
  266.1 1.8 fusion
  267.8 3.9 convert_element_type.94
  271.7 7.5 %all-to-all-start.3 = ((bf16[64,4,3072]{2,1,0:T(4,128)(2,1)}), bf16[64,4,3072]{2,1,0:T(4,128)(2,1)}, u32[]{:S(2)}, u32[]{:S(2)}) async-start(bf16[64,4,3072]{2,1,0:T(4,128)(2,1)} %convert_element_type.94), calls=%async_computation.3 | async-start | bytes 3145728 | tf_op jit(solution)/shard_map/all_to_all | solution.py:86
  279.4 0.7 select_reduce_fusion.2
  280.1 1.5 fusion.2
  281.6 1.3 fusion.3
  282.9 70.8 %all-to-all-done.3 = bf16[64,4,3072]{2,1,0:T(4,128)(2,1)} async-done(((bf16[64,4,3072]{2,1,0:T(4,128)(2,1)}), bf16[64,4,3072]{2,1,0:T(4,128)(2,1)}, u32[]{:S(2)}, u32[]{:S(2)}) %all-to-all-start.3) | async-done | bytes 1572896 | tf_op jit(solution)/shard_map/all_to_all | solution.py:86
  353.6 2.2 convert_reduce_fusion
  355.8 0.4 fusion.4
  356.2 1.2 copy.46
  357.4 1.5 fusion.1
  358.9 27.2 %reduce-scatter.4.cloned.1.call-done = bf16[384,8]{1,0:T(8,128)(2,1)} async-done(((bf16[3072,8]{1,0:T(8,128)(2,1)}), bf16[384,8]{1,0:T(8,128)(2,1)}) %reduce-scatter.4.cloned.1.call-update) | async-done | bytes 6160
  386.1 1.6 copy.47
  (31 shorter events, 0.6 us)
Async XLA Ops:
  7.2 124.1 %copy-start = (bf16[1,3072,128]{2,1,0:T(8,128)(2,1)S(1)}, bf16[1,3072,128]{2,1,0:T(8,128)(2,1)}, u32[]{:S(2)}) copy-start(bf16[1,3072,128]{2,1,0:T(8,128)(2,1)} %param.11) | copy-start | bytes 2359300
  23.7 18.8 %copy-start.6 = (bf16[8,384]{1,0:T(8,128)(2,1)S(1)}, bf16[8,384]{1,0:T(8,128)(2,1)}, u32[]{:S(2)}) copy-start(bf16[8,384]{1,0:T(8,128)(2,1)} %param.8) | copy-start | bytes 18436
  23.7 96.9 %all-to-all-start.2 = ((bf16[64,4,3072]{2,1,0:T(4,128)(2,1)}), bf16[64,4,3072]{2,1,0:T(4,128)(2,1)S(1)}, u32[]{:S(2)}, u32[]{:S(2)}) async-start(bf16[64,4,3072]{2,1,0:T(4,128)(2,1)} %bitcast.54), calls=%async_computation.2 | async-start | bytes 3145728 | tf_op jit(solution)/shard_map/all_to_all | solution.py:58
  120.6 1.7 copy-start.2
  122.2 6.2 %copy-start.7 = (bf16[8,2]{0,1:T(2,128)(2,1)S(1)}, bf16[8,2]{0,1:T(2,128)(2,1)}, u32[]{:S(2)}) copy-start(bf16[8,2]{0,1:T(2,128)(2,1)} %param.9) | copy-start | bytes 100
  122.2 83.6 %all-to-all-start.1 = ((bf16[64,4,3072]{2,1,0:T(4,128)(2,1)}), bf16[64,4,3072]{2,1,0:T(4,128)(2,1)}, u32[]{:S(2)}, u32[]{:S(2)}) async-start(bf16[64,4,3072]{2,1,0:T(4,128)(2,1)} %bitcast.55), calls=%async_computation.1 | async-start | bytes 3145728 | tf_op jit(solution)/shard_map/all_to_all | solution.py:59
  131.3 1.1 copy-start.3
  209.5 23.0 %copy-start.4 = (s32[8,2]{0,1:T(2,128)S(1)}, s32[8,2]{0,1:T(2,128)}, u32[]{:S(2)}) copy-start(s32[8,2]{0,1:T(2,128)} %param.10) | copy-start | bytes 196
  225.6 19.7 %all-to-all-start.4 = ((bf16[64,1,4]{2,1,0:T(2,128)(2,1)}), bf16[64,1,4]{2,1,0:T(2,128)(2,1)S(1)}, u32[]{:S(2)}, u32[]{:S(2)}) async-start(bf16[64,1,4]{2,1,0:T(2,128)(2,1)} %convert_element_type.106), calls=%async_computation.4 | async-start | bytes 65536 | tf_op jit(solution)/shard_map/all_to_all | solution.py:93
  271.7 7.7 %copy-start.5 = (s32[8,2]{0,1:T(2,128)S(1)}, s32[8,2]{0,1:T(2,128)}, u32[]{:S(2)}) copy-start(s32[8,2]{0,1:T(2,128)} %param.10) | copy-start | bytes 196
  271.7 82.0 %all-to-all-start.3 = ((bf16[64,4,3072]{2,1,0:T(4,128)(2,1)}), bf16[64,4,3072]{2,1,0:T(4,128)(2,1)}, u32[]{:S(2)}, u32[]{:S(2)}) async-start(bf16[64,4,3072]{2,1,0:T(4,128)(2,1)} %convert_element_type.94), calls=%async_computation.3 | async-start | bytes 3145728 | tf_op jit(solution)/shard_map/all_to_all | solution.py:86
  279.2 106.9 %reduce-scatter.4.cloned.1.call-start = ((), (), s32[]{:S(2)}) async-start(), calls=%async_computation.6 | async-start | bytes 884736
  279.3 2.2 copy-start.1
Sparse Core Ops, SparseCore 0:
  357.5 28.5 reduce-scatter.3
where the time goes:
time: 395 us
  waiting for transfers between devices  248 us (63%)
  blocking collectives  57 us (14%)
  starting transfers between devices  39.4 us (10%)
  local copies, waits for them, and re-layouts  18.6 us (5%)
  between operations  14.2 us (4%)
  matrix products  11.6 us (3%)
  other arithmetic  5.14 us (1%)
    all_to_all x1, waiting for transfers between devices, shards(): lax.all_to_all(spread(select(full_up)), 'wide', split_axis=0, concat_axis...  72.8 us
    all_to_all x1, waiting for transfers between devices, shards(): lax.all_to_all(returned.reshape(n_wide, CAP, feature_width).astype(jnp.bf...  70.8 us
    all_to_all x1, waiting for transfers between devices, shards(): lax.all_to_all(spread(select(full_in)), 'wide', split_axis=0, concat_axis...  65.1 us
    unnamed x2, waiting for transfers between devices  27.2 us
    all_to_all x1, starting transfers between devices, shards(): lax.all_to_all(spread(select(full_in)), 'wide', split_axis=0, concat_axis...  18.7 us
    all_to_all x1, blocking collectives, shards(): lax.all_to_all(gate_sent, 'wide', split_axis=0, concat_axis=0, tiled=True)  18.4 us
    all_gather x1, blocking collectives, shards(): lax.all_gather(tokens, 'tensor', axis=1, tiled=True)  13.4 us
    all_gather x1, blocking collectives, shards(): lax.all_gather(cotangent, 'tensor', axis=1, tiled=True)  12.8 us
  transfers between devices with their start and end apart: 5, of which 5 were waited for; matrix products, arithmetic and copies ran while one was open for 2% of the time, Pallas kernels for 0%

commit v1 on v0

v1 whole, which is shorter than its diff:
```python
import jax
import jax.numpy as jnp
from jax import lax
from jax.experimental import pallas as pl
from jax.experimental.pallas import tpu as pltpu
from jax.sharding import PartitionSpec as P

MESH = pl.DeviceIdType.MESH
NZ, NY, NX = 16, 4, 4
TOK = 8
D = 3072
FEAT = 384
HID = 128
ROWS = 64
SLOTS = 256
BF = jnp.bfloat16
F32 = jnp.float32
VMEM = pl.BlockSpec(memory_space=pltpu.VMEM)


def position():
    tensor, wide = lax.axis_index("tensor"), lax.axis_index("wide")
    return (
        lax.div(tensor, 2),
        lax.rem(tensor, 2),
        lax.div(wide, NY),
        lax.rem(wide, NY),
    )


def device_of(x, core, z, y):
    return {"tensor": x * 2 + core, "wide": z * NY + y}


def wrap(value, size):
    return lax.rem(value + size, size)


def dot(left, right, left_dim, right_dim):
    return lax.dot_general(
        left, right, (((left_dim,), (right_dim,)), ((), ())), preferred_element_type=F32
    )


def meet(partners):
    barrier = pltpu.get_barrier_semaphore()
    for partner in partners:
        pl.semaphore_signal(barrier, inc=1, device_id=partner, device_id_type=MESH)
    pl.semaphore_wait(barrier, len(partners))


class Wire:
    def __init__(self, send_sem, recv_sem):
        self.send_sem, self.recv_sem = send_sem, recv_sem
        self.sent = []

    def make(self, number, source, target, device):
        return pltpu.make_async_remote_copy(
            src_ref=source,
            dst_ref=target,
            send_sem=self.send_sem.at[number],
            recv_sem=self.recv_sem.at[number],
            device_id=device,
            device_id_type=MESH,
        )

    def send(self, number, source, target, device):
        copy = self.make(number, source, target, device)
        copy.start()
        self.sent.append(copy)

    def arrived(self, number, landed, device):
        self.make(number, landed, landed, device).wait_recv()

    def drain(self):
        for copy in self.sent:
            copy.wait_send()


def slot_match(experts, lanes, per_expert):
    lane = lax.broadcasted_iota(jnp.int32, (TOK, lanes), 1)
    expert, half, slot = lane // per_expert, (lane // 4) % 2, lane % 4
    first = jnp.broadcast_to(experts[:, 0:1], (TOK, lanes)) == expert
    second = jnp.broadcast_to(experts[:, 1:2], (TOK, lanes)) == expert
    one, zero = jnp.ones((TOK, lanes), F32), jnp.zeros((TOK, lanes), F32)
    first, second = jnp.where(first, one, zero), jnp.where(second, one, zero)
    row = lax.broadcasted_iota(jnp.int32, (TOK, TOK), 0)
    column = lax.broadcasted_iota(jnp.int32, (TOK, TOK), 1)
    earlier = jnp.where(column < row, 1.0, 0.0).astype(F32)
    before = dot(earlier, first + second, 1, 0)
    at_slot = jnp.where(before == slot.astype(F32), one, zero)
    upper = jnp.where(half == 0, one, zero)
    return first * at_slot, second * at_slot, upper


def dispatch_kernel(
    tokens_ref,
    cotangent_ref,
    gates_ref,
    experts_ref,
    x_ref,
    c_ref,
    g_ref,
    out_buf,
    in_buf,
    z_send,
    z_recv,
    send_sem,
    recv_sem,
):
    x, core, z, y = position()
    peers_z = [device_of(x, core, wrap(z + d, NZ), y) for d in range(1, NZ)]
    x_next, x_prev = device_of(wrap(x + 1, NX), core, z, y), device_of(wrap(x - 1, NX), core, z, y)
    y_next, y_prev = device_of(x, core, z, wrap(y + 1, NY)), device_of(x, core, z, wrap(y - 1, NY))
    y_far = device_of(x, core, z, wrap(y + 2, NY))
    sibling = device_of(x, 1 - core, z, y)
    meet(peers_z + [x_next, x_prev, y_next, y_prev, y_far, sibling])

    first, second, upper = slot_match(experts_ref[...], 64, 8)
    gates = gates_ref[...].astype(F32)
    either = first + second
    pick_in = (either * upper).astype(BF)
    pick_up = (either * (1.0 - upper)).astype(BF)
    chosen = dot(pick_in, tokens_ref[...], 0, 0) + dot(pick_up, cotangent_ref[...], 0, 0)
    gate_at = first * gates[:, 0:1] + second * gates[:, 1:2]
    gate_rows = dot(gate_at.astype(BF), jnp.ones((TOK, 128), BF), 0, 0)
    out_buf[:, :, 0:FEAT] = chosen.reshape(8, 8, FEAT).astype(BF)
    out_buf[:, :, FEAT:] = gate_rows.reshape(8, 8, 128).astype(BF)

    zwire = Wire(z_send, z_recv)
    for d in (8, 7, 9, 6, 10, 5, 11, 4, 12, 3, 13, 2, 14, 1, 15):
        there = wrap(z + d, NZ)
        zwire.send(
            d - 1, out_buf.at[lax.div(there, 2)], in_buf.at[z], device_of(x, core, there, y)
        )
    in_buf[z] = out_buf[lax.div(z, 2)]
    for d in range(1, NZ):
        zwire.arrived(d - 1, in_buf.at[wrap(z - d, NZ)], sibling)

    out_row = lax.broadcasted_iota(jnp.int32, (128, 128), 0)
    in_row = lax.broadcasted_iota(jnp.int32, (128, 128), 1)
    wanted = (out_row % 64) // 4 * 8 + out_row // 64 * 4 + out_row % 4
    order = jnp.where(in_row == wanted, 1.0, 0.0).astype(BF)
    came = in_buf[...].astype(F32).reshape(128, FEAT + 128).astype(BF)
    sorted_rows = dot(order, came, 1, 0).astype(BF)

    def block(ref, xi, ci, yi, start=0, count=ROWS):
        return ref.at[
            pl.ds(pl.multiple_of(yi * ROWS + start, 32), count),
            pl.ds(pl.multiple_of((xi * 2 + ci) * FEAT, 128), FEAT),
        ]

    my_rows = pl.ds(pl.multiple_of(y * ROWS, ROWS), ROWS)
    my_columns = pl.ds(pl.multiple_of((x * 2 + core) * FEAT, 128), FEAT)
    x_ref[my_rows, my_columns] = sorted_rows[0:64, 0:FEAT]
    c_ref[my_rows, my_columns] = sorted_rows[64:128, 0:FEAT]
    g_ref[my_rows, :] = sorted_rows[0:64, FEAT:]

    wire = Wire(send_sem, recv_sem)

    class Gather:
        def __init__(self, ref, base, first_axis):
            self.ref, self.base = ref, base
            if first_axis == "x":
                self.a, self.b = x, y
                self.up, self.down, self.fore, self.back = x_next, x_prev, y_next, y_prev
            else:
                self.a, self.b = y, x
                self.up, self.down, self.fore, self.back = y_next, y_prev, x_next, x_prev
            self.swap = first_axis != "x"

        def at(self, a, b, ci, start=0, count=ROWS):
            a, b = wrap(self.a + a, 4), wrap(self.b + b, 4)
            xi, yi = (b, a) if self.swap else (a, b)
            return block(self.ref, xi, ci, yi, start, count)

        def push(self, number, piece, device):
            wire.send(self.base + number, piece, piece, device)

        def got(self, number, piece):
            wire.arrived(self.base + number, piece, sibling)

        def start(self):
            own = self.at(0, 0, core)
            self.push(0, own, self.up)
            self.push(1, own, self.down)

        def spread(self, k, a):
            own = self.at(a, 0, core)
            self.push(4 + 4 * k, own, self.fore)
            self.push(5 + 4 * k, own, self.back)
            self.push(20 + 4 * k, own, sibling)

        def first_near(self):
            self.got(0, self.at(-1, 0, core))
            self.push(2, self.at(-1, 0, core, 0, 32), self.up)
            self.spread(1, -1)
            self.got(1, self.at(1, 0, core))
            self.push(3, self.at(1, 0, core, 32, 32), self.down)
            self.spread(2, 1)

        def first_far(self):
            self.got(2, self.at(2, 0, core, 0, 32))
            self.got(3, self.at(2, 0, core, 32, 32))
            self.spread(3, 2)

        def second_near(self, k, a):
            self.got(4 + 4 * k, self.at(a, -1, core))
            self.push(6 + 4 * k, self.at(a, -1, core, 0, 32), self.fore)
            self.push(21 + 4 * k, self.at(a, -1, core), sibling)
            self.got(5 + 4 * k, self.at(a, 1, core))
            self.push(7 + 4 * k, self.at(a, 1, core, 32, 32), self.back)
            self.push(22 + 4 * k, self.at(a, 1, core), sibling)

        def second_far(self, k, a):
            self.got(6 + 4 * k, self.at(a, 2, core, 0, 32))
            self.got(7 + 4 * k, self.at(a, 2, core, 32, 32))
            self.push(23 + 4 * k, self.at(a, 2, core), sibling)

        def from_sibling(self):
            for k, a in enumerate((0, -1, 1, 2)):
                for m, b in enumerate((0, -1, 1, 2)):
                    self.got(20 + 4 * k + m, self.at(a, b, 1 - core))

    gathers = (Gather(x_ref, 0, "x"), Gather(c_ref, 36, "y"))
    for one in gathers:
        one.start()
    for one in gathers:
        one.spread(0, 0)
    gate_block = g_ref.at[my_rows, :]
    for number, device in enumerate((y_next, y_prev, y_far)):
        wire.send(72 + number, gate_block, gate_block, device)
    for one in gathers:
        one.first_near()
    for one in gathers:
        one.second_near(0, 0)
    for one in gathers:
        one.first_far()
    for k, a in ((1, -1), (2, 1)):
        for one in gathers:
            one.second_near(k, a)
        for one in gathers:
            one.second_far(k - 1, (0, -1)[k - 1])
    for one in gathers:
        one.second_near(3, 2)
    for one in gathers:
        one.second_far(2, 1)
    for one in gathers:
        one.second_far(3, 2)
    for one in gathers:
        one.from_sibling()
    for number, d in enumerate((-1, 1, 2)):
        landed = g_ref.at[pl.ds(pl.multiple_of(wrap(y + d, NY) * ROWS, ROWS), ROWS), :]
        wire.arrived(72 + number, landed, sibling)
    zwire.drain()
    wire.drain()


def dispatch(tokens, cotangent, gates, experts):
    return pl.pallas_call(
        dispatch_kernel,
        name="dispatch",
        out_shape=(
            jax.ShapeDtypeStruct((SLOTS, D), BF),
            jax.ShapeDtypeStruct((SLOTS, D), BF),
            jax.ShapeDtypeStruct((SLOTS, 128), BF),
        ),
        in_specs=[VMEM] * 4,
        out_specs=(VMEM,) * 3,
        scratch_shapes=[
            pltpu.VMEM((8, 8, FEAT + 128), BF),
            pltpu.VMEM((NZ, 8, FEAT + 128), BF),
            pltpu.SemaphoreType.DMA((NZ - 1,)),
            pltpu.SemaphoreType.DMA((NZ - 1,)),
            pltpu.SemaphoreType.DMA((75,)),
            pltpu.SemaphoreType.DMA((75,)),
        ],
        compiler_params=pltpu.CompilerParams(
            collective_id=0, has_side_effects=True, vmem_limit_bytes=24 << 20
        ),
    )(tokens, cotangent, gates, experts)


def layer_kernel(
    x_ref, c_ref, g_ref, wg_ref, wu_ref, wd_ref, dwg_ref, dwu_ref, dwd_ref, r_ref, t_ref
):
    scale = g_ref[...].astype(F32)
    pre_gate = dot(x_ref[...], wg_ref[0], 1, 0)
    pre_up = dot(x_ref[...], wu_ref[0], 1, 0)
    through = dot(c_ref[...], wd_ref[0], 1, 1)
    sig = jax.nn.sigmoid(pre_gate)
    act = pre_gate * sig
    hidden = act * pre_up
    weighted = (scale * hidden).astype(BF)
    hidden_grad = scale * through
    grad_gate = (hidden_grad * pre_up * sig * (1.0 + pre_gate * (1.0 - sig))).astype(BF)
    grad_up = (hidden_grad * act).astype(BF)

    row = lax.broadcasted_iota(jnp.int32, (ROWS, 128), 0)
    lane = lax.broadcasted_iota(jnp.int32, (ROWS, 128), 1)
    sums = jnp.sum(through * hidden, axis=1, keepdims=True)
    for yi in range(NY):
        part = jnp.broadcast_to(sums[yi * ROWS : (yi + 1) * ROWS], (ROWS, 128))
        line = jnp.sum(jnp.where(row == lane, part, 0.0), axis=0, keepdims=True)
        t_ref[yi] = jnp.broadcast_to(line, (8, 128))

    step = 512
    for k in range(D // step):
        rows = pl.ds(k * step, step)
        r_ref[:, rows] = (
            dot(grad_gate, wg_ref[0, rows, :], 1, 1) + dot(grad_up, wu_ref[0, rows, :], 1, 1)
        ).astype(BF)
        dwg_ref[0, rows, :] = dot(x_ref[:, rows], grad_gate, 0, 0).astype(BF)
        dwu_ref[0, rows, :] = dot(x_ref[:, rows], grad_up, 0, 0).astype(BF)
        dwd_ref[0, :, rows] = dot(weighted, c_ref[:, rows], 0, 0).astype(BF)


def layer(inputs, upstream, scale, w_gate, w_up, w_down):
    return pl.pallas_call(
        layer_kernel,
        name="layer",
        out_shape=(
            jax.ShapeDtypeStruct((1, D, HID), BF),
            jax.ShapeDtypeStruct((1, D, HID), BF),
            jax.ShapeDtypeStruct((1, HID, D), BF),
            jax.ShapeDtypeStruct((SLOTS, D), BF),
            jax.ShapeDtypeStruct((NY, 8, 128), F32),
        ),
        in_specs=[VMEM] * 6,
        out_specs=(VMEM,) * 5,
        compiler_params=pltpu.CompilerParams(vmem_limit_bytes=40 << 20),
    )(inputs, upstream, scale, w_gate, w_up, w_down)


def combine_kernel(
    r_ref,
    t_ref,
    experts_ref,
    grad_ref,
    routing_ref,
    sib_buf,
    acc_p,
    acc_q,
    near_p,
    near_q,
    full_p,
    full_q,
    mid_p,
    mid_q,
    last_p,
    last_q,
    t_y,
    t_sum,
    t_t,
    out_buf,
    in_buf,
    z_send,
    z_recv,
    send_sem,
    recv_sem,
):
    x, core, z, y = position()
    tensor = x * 2 + core
    peers_z = [device_of(x, core, wrap(z + d, NZ), y) for d in range(1, NZ)]
    peers_t = [{"tensor": wrap(tensor + d, 8), "wide": z * NY + y} for d in range(1, 8)]
    peers_y = [device_of(x, core, z, wrap(y + d, NY)) for d in range(1, NY)]
    peers_x = [device_of(wrap(x + d, NX), core, z, y) for d in range(1, NX)]
    sibling = device_of(x, 1 - core, z, y)
    meet(peers_z + peers_t + peers_y)

    wire = Wire(send_sem, recv_sem)
    x_order = (2, 1, 3, 0)
    for k, d in enumerate(x_order):
        xi = wrap(x + d, NX)
        columns = pl.ds(pl.multiple_of((xi * 2 + 1 - core) * FEAT, 128), FEAT)
        wire.send(k, r_ref.at[:, columns], sib_buf.at[k], sibling)
    for d in range(1, NY):
        wire.send(3 + d, t_ref.at[wrap(y + d, NY)], t_y.at[d - 1], peers_y[d - 1])

    for k, d in enumerate(x_order):
        xi = wrap(x + d, NX)
        columns = pl.ds(pl.multiple_of((xi * 2 + core) * FEAT, 128), FEAT)
        wire.arrived(k, sib_buf.at[k], sibling)
        for yi in range(NY):
            rows = pl.ds(yi * ROWS, ROWS)
            total = (
                r_ref[rows, columns].astype(F32) + sib_buf[k, rows, :].astype(F32)
            ).astype(BF)
            acc_p[xi, yi] = total[0:32]
            acc_q[yi, xi] = total[32:64]

    class Scatter:
        def __init__(self, base, acc, near, full, mid, last, a, b, first_peers, second_peers):
            self.base, self.acc, self.near, self.full = base, acc, near, full
            self.mid, self.last, self.a, self.b = mid, last, a, b
            self.first_peers, self.second_peers = first_peers, second_peers

        def far(self):
            far = wrap(self.a + 2, 4)
            wire.send(
                self.base, self.acc.at[far, pl.ds(0, 2)], self.near.at[0], self.first_peers[0]
            )
            wire.send(
                self.base + 1, self.acc.at[far, pl.ds(2, 2)], self.near.at[1], self.first_peers[2]
            )

        def close(self):
            for side, chunk, peer in ((0, 1, 0), (1, 3, 2)):
                wire.arrived(self.base + side, self.near.at[side], sibling)
                there = wrap(self.a + chunk, 4)
                for i in range(2):
                    self.acc[there, 2 * side + i] = (
                        self.acc[there, 2 * side + i].astype(F32)
                        + self.near[side, i].astype(F32)
                    ).astype(BF)
                wire.send(
                    self.base + 2 + side,
                    self.acc.at[there],
                    self.full.at[side],
                    self.first_peers[peer],
                )

        def across(self):
            for side in range(2):
                wire.arrived(self.base + 2 + side, self.full.at[side], sibling)
            for i in range(4):
                self.mid[i] = (
                    self.acc[self.a, i].astype(F32)
                    + self.full[0, i].astype(F32)
                    + self.full[1, i].astype(F32)
                ).astype(BF)
            for d in range(1, 4):
                wire.send(
                    self.base + 3 + d,
                    self.mid.at[wrap(self.b + d, 4)],
                    self.last.at[d - 1],
                    self.second_peers[d - 1],
                )

        def total(self):
            result = self.mid[self.b].astype(F32)
            for d in range(1, 4):
                wire.arrived(self.base + 3 + d, self.last.at[d - 1], sibling)
                result = result + self.last[d - 1].astype(F32)
            return result

    scatters = (
        Scatter(7, acc_p, near_p, full_p, mid_p, last_p, x, y, peers_x, peers_y),
        Scatter(14, acc_q, near_q, full_q, mid_q, last_q, y, x, peers_y, peers_x),
    )
    for one in scatters:
        one.far()
    line = t_ref[y]
    for d in range(1, NY):
        wire.arrived(3 + d, t_y.at[d - 1], sibling)
        line = line + t_y[d - 1]
    t_sum[...] = line
    t_t[tensor] = line
    for d in range(1, 8):
        wire.send(20 + d, t_sum, t_t.at[tensor], peers_t[d - 1])
    for one in scatters:
        one.close()
    for one in scatters:
        one.across()
    for d in range(1, 8):
        wire.arrived(20 + d, t_t.at[wrap(tensor - d, 8)], sibling)
    line = t_t[0]
    for i in range(1, 8):
        line = line + t_t[i]
    row = lax.broadcasted_iota(jnp.int32, (ROWS, 128), 0)
    lane = lax.broadcasted_iota(jnp.int32, (ROWS, 128), 1)
    spread = jnp.where(row == lane, jnp.broadcast_to(line[0:1], (ROWS, 128)), 0.0)
    column = jnp.broadcast_to(jnp.sum(spread, axis=1, keepdims=True), (ROWS, 128))

    result = jnp.concatenate([one.total() for one in scatters], axis=0)
    pair = jnp.concatenate(
        [
            result[:, 0:256],
            jnp.concatenate([result[:, 256:FEAT], column], axis=1),
        ],
        axis=0,
    ).astype(BF)
    out_row = lax.broadcasted_iota(jnp.int32, (128, 128), 0)
    in_row = lax.broadcasted_iota(jnp.int32, (128, 128), 1)
    wanted = (out_row // 4) % 2 * 64 + out_row // 8 * 4 + out_row % 4
    order = jnp.where(in_row == wanted, 1.0, 0.0).astype(BF)
    out_buf[...] = dot(order, pair, 1, 0).reshape(NZ, 8, 256).astype(BF)

    zwire = Wire(z_send, z_recv)
    for d in (8, 7, 9, 6, 10, 5, 11, 4, 12, 3, 13, 2, 14, 1, 15):
        zwire.send(d - 1, out_buf.at[wrap(z + d, NZ)], in_buf.at[z], peers_z[d - 1])
    in_buf[z] = out_buf[z]
    first, second, upper = slot_match(experts_ref[...], 128, 16)
    for d in range(1, NZ):
        zwire.arrived(d - 1, in_buf.at[wrap(z - d, NZ)], sibling)
    came = in_buf[...].astype(F32).reshape(128, 256).astype(BF)
    either = first + second
    lower = 1.0 - upper
    head = dot((either * upper).astype(BF), came, 1, 0)
    tail = dot((either * lower).astype(BF), came[:, 0:128], 1, 0)
    grad_ref[:, 0:256] = head.astype(BF)
    grad_ref[:, 256:FEAT] = tail.astype(BF)
    at_first = dot((first * lower).astype(BF), came[:, 128:], 1, 0)
    at_second = dot((second * lower).astype(BF), came[:, 128:], 1, 0)
    which = lax.broadcasted_iota(jnp.int32, (TOK, 128), 1)
    routing_ref[...] = jnp.where(which == 0, at_first, at_second)[:, 0:2]
    zwire.drain()
    wire.drain()


def combine(returned, lines, experts):
    return pl.pallas_call(
        combine_kernel,
        name="combine",
        out_shape=(
            jax.ShapeDtypeStruct((TOK, FEAT), BF),
            jax.ShapeDtypeStruct((TOK, 2), F32),
        ),
        in_specs=[VMEM] * 3,
        out_specs=(VMEM,) * 2,
        scratch_shapes=[
            pltpu.VMEM((NX, SLOTS, FEAT), BF),
            pltpu.VMEM((4, 4, 32, FEAT), BF),
            pltpu.VMEM((4, 4, 32, FEAT), BF),
            pltpu.VMEM((2, 2, 32, FEAT), BF),
            pltpu.VMEM((2, 2, 32, FEAT), BF),
            pltpu.VMEM((2, 4, 32, FEAT), BF),
            pltpu.VMEM((2, 4, 32, FEAT), BF),
            pltpu.VMEM((4, 32, FEAT), BF),
            pltpu.VMEM((4, 32, FEAT), BF),
            pltpu.VMEM((3, 32, FEAT), BF),
            pltpu.VMEM((3, 32, FEAT), BF),
            pltpu.VMEM((3, 8, 128), F32),
            pltpu.VMEM((8, 128), F32),
            pltpu.VMEM((8, 8, 128), F32),
            pltpu.VMEM((NZ, 8, 256), BF),
            pltpu.VMEM((NZ, 8, 256), BF),
            pltpu.SemaphoreType.DMA((NZ - 1,)),
            pltpu.SemaphoreType.DMA((NZ - 1,)),
            pltpu.SemaphoreType.DMA((28,)),
            pltpu.SemaphoreType.DMA((28,)),
        ],
        compiler_params=pltpu.CompilerParams(
            collective_id=1, has_side_effects=True, vmem_limit_bytes=24 << 20
        ),
    )(returned, lines, experts)


def shards(tokens, cotangent, gates, experts, w_gate, w_up, w_down):
    inputs, upstream, scale = dispatch(tokens, cotangent, gates, experts)
    gate_grad, up_grad, down_grad, returned, lines = layer(
        inputs, upstream, scale, w_gate, w_up, w_down
    )
    input_grad, routing_grad = combine(returned, lines, experts)
    return input_grad, routing_grad, gate_grad, up_grad, down_grad


def solution(mesh):
    return jax.shard_map(
        shards,
        mesh=mesh,
        in_specs=(
            P("wide", "tensor"),
            P("wide", "tensor"),
            P("wide", None),
            P("wide", None),
            P("wide", None, "tensor"),
            P("wide", None, "tensor"),
            P("wide", "tensor", None),
        ),
        out_specs=(
            P("wide", "tensor"),
            P("wide", None),
            P("wide", None, "tensor"),
            P("wide", None, "tensor"),
            P("wide", "tensor", None),
        ),
        check_vma=False,
    )
```

time: 395 us -> 85.6 us (0.22)
  the two profiles are of different devices: /device:TPU:16 before, /device:TPU:4 now
where the time goes in v1:
time: 85.6 us; the launch traced here: 85.2 us
  Pallas kernels  77 us (90%)
  local copies, waits for them, and re-layouts  7.5 us (9%)
    pallas_call x1, Pallas kernels, dispatch(): pl.pallas_call(dispatch_kernel, name='dispatch', out_shape=(jax.ShapeDtyp...  42.5 us
    pallas_call x1, Pallas kernels, combine(): pl.pallas_call(combine_kernel, name='combine', out_shape=(jax.ShapeDtypeS...  29.2 us
    unnamed x14, local copies, waits for them, and re-layouts  7.5 us
    pallas_call x1, Pallas kernels, layer(): pl.pallas_call(layer_kernel, name='layer', out_shape=(jax.ShapeDtypeStruc...  5.31 us

profile of v1, /device:TPU:4, one launch (start us, length us, event | category | flops | bytes accessed | tf_op | source)
XLA Modules:
  0.0 85.2 jit_solution(12282528058761716840)
XLA Ops:
  0.6 0.7 copy.12.gates_ref
  1.4 0.8 copy.13.experts_ref
  2.1 0.0 copy-start.3
  2.1 0.7 copy-done.3
  2.8 0.0 copy-start.4
  2.8 0.7 copy-done.4
  3.5 42.5 %dispatch.1 = (bf16[256,3072]{1,0:T(8,128)(2,1)S(1)}, bf16[256,3072]{1,0:T(8,128)(2,1)S(1)}, bf16[256,128]{1,0:T(8,128)(2,1)S(1)}) custom-call(bf16[8,384]{1,0:T(8,128)(2,1)S(1)} %copy-done.3, bf16[8,384]{1,0:T(8,128)(2,1)S(1)} %copy-done.4, bf16[8,2]{1,0:T(8,128)(2,1)S(1)} %copy.12.gates_ref, s32[8,2]{1,0:T(8,128)S(1)} %copy.13.experts_ref), custom_call_target="tpu_custom_call" | custom-call | tf_op jit(solution)/shard_map/dispatch/pallas_call | solution.py:260
  46.0 0.0 copy-start
  46.1 1.1 %copy-done = bf16[1,3072,128]{2,1,0:T(8,128)(2,1)S(1)} copy-done((bf16[1,3072,128]{2,1,0:T(8,128)(2,1)S(1)}, bf16[1,3072,128]{2,1,0:T(8,128)(2,1)}, u32[]{:S(2)}) %copy-start) | copy-done | bytes 786456
  47.2 0.0 copy-start.1
  47.2 1.1 %copy-done.1 = bf16[1,3072,128]{2,1,0:T(8,128)(2,1)S(1)} copy-done((bf16[1,3072,128]{2,1,0:T(8,128)(2,1)S(1)}, bf16[1,3072,128]{2,1,0:T(8,128)(2,1)}, u32[]{:S(2)}) %copy-start.1) | copy-done | bytes 786456
  48.3 0.0 copy-start.2
  48.3 1.1 %copy-done.2 = bf16[1,128,3072]{2,1,0:T(8,128)(2,1)S(1)} copy-done((bf16[1,128,3072]{2,1,0:T(8,128)(2,1)S(1)}, bf16[1,128,3072]{2,1,0:T(8,128)(2,1)}, u32[]{:S(2)}) %copy-start.2) | copy-done | bytes 786456
  49.5 5.3 %layer.1 = (bf16[1,3072,128]{2,1,0:T(8,128)(2,1)}, bf16[1,3072,128]{2,1,0:T(8,128)(2,1)}, bf16[1,128,3072]{2,1,0:T(8,128)(2,1)}, bf16[256,3072]{1,0:T(8,128)(2,1)S(1)}, f32[4,8,128]{2,1,0:T(8,128)S(1)}) custom-call(bf16[256,3072]{1,0:T(8,128)(2,1)S(1)} %get-tuple-element.15.x_ref, bf16[256,3072]{1,0:T(8,128)(2,1)S(1)} %get-tuple-element.16.c_ref, ...), custom_call_target="tpu_custom_call" | custom-call | tf_op jit(solution)/shard_map/layer/pallas_call | solution.py:319
  54.8 29.2 %combine.1 = (bf16[8,384]{1,0:T(8,128)(2,1)S(1)}, f32[8,2]{1,0:T(8,128)S(1)}) custom-call(bf16[256,3072]{1,0:T(8,128)(2,1)S(1)} %get-tuple-element.18.r_ref, f32[4,8,128]{2,1,0:T(8,128)S(1)} %get-tuple-element.19.t_ref, s32[8,2]{1,0:T(8,128)S(1)} %copy.13.experts_ref), custom_call_target="tpu_custom_call" | custom-call | tf_op jit(solution)/shard_map/combine/pallas_call | solution.py:512
  84.0 0.6 copy.15
  84.6 0.6 copy.17
Async XLA Ops:
  2.1 0.7 copy-start.3
  2.8 0.7 copy-start.4
  46.0 1.1 %copy-start = (bf16[1,3072,128]{2,1,0:T(8,128)(2,1)S(1)}, bf16[1,3072,128]{2,1,0:T(8,128)(2,1)}, u32[]{:S(2)}) copy-start(bf16[1,3072,128]{2,1,0:T(8,128)(2,1)} %wg_ref.1) | copy-start | bytes 2359300
  47.2 1.1 %copy-start.1 = (bf16[1,3072,128]{2,1,0:T(8,128)(2,1)S(1)}, bf16[1,3072,128]{2,1,0:T(8,128)(2,1)}, u32[]{:S(2)}) copy-start(bf16[1,3072,128]{2,1,0:T(8,128)(2,1)} %wu_ref.1) | copy-start | bytes 2359300
  48.3 1.1 %copy-start.2 = (bf16[1,128,3072]{2,1,0:T(8,128)(2,1)S(1)}, bf16[1,128,3072]{2,1,0:T(8,128)(2,1)}, u32[]{:S(2)}) copy-start(bf16[1,128,3072]{2,1,0:T(8,128)(2,1)} %wd_ref.1) | copy-start | bytes 2359300

commit v2 on v0

v2 whole, which is shorter than its diff:
```python
import jax
import jax.numpy as jnp
from jax import lax
from jax.experimental import pallas as pl
from jax.experimental.pallas import tpu as pltpu
from jax.sharding import PartitionSpec as P

MESH = pl.DeviceIdType.MESH
NZ, NY, NX = 16, 4, 4
TOK = 8
D = 3072
FEAT = 384
HID = 128
ROWS = 64
SLOTS = 256
BF = jnp.bfloat16
F32 = jnp.float32
VMEM = pl.BlockSpec(memory_space=pltpu.VMEM)
HBM = pl.BlockSpec(memory_space=pltpu.MemorySpace.HBM)
Z_ORDER = (8, 7, 9, 6, 10, 5, 11, 4, 12, 3, 13, 2, 14, 1, 15)


def position():
    tensor, wide = lax.axis_index("tensor"), lax.axis_index("wide")
    return (
        lax.div(tensor, 2),
        lax.rem(tensor, 2),
        lax.div(wide, NY),
        lax.rem(wide, NY),
    )


def device_of(x, core, z, y):
    return {"tensor": x * 2 + core, "wide": z * NY + y}


def wrap(value, size):
    return lax.rem(value + size, size)


def dot(left, right, left_dim, right_dim):
    return lax.dot_general(
        left, right, (((left_dim,), (right_dim,)), ((), ())), preferred_element_type=F32
    )


class Wire:
    def __init__(self, send_sem, recv_sem):
        self.send_sem, self.recv_sem = send_sem, recv_sem
        self.sent = []

    def make(self, number, source, target, device):
        return pltpu.make_async_remote_copy(
            src_ref=source,
            dst_ref=target,
            send_sem=self.send_sem.at[number],
            recv_sem=self.recv_sem.at[number],
            device_id=device,
            device_id_type=MESH,
        )

    def send(self, number, source, target, device):
        copy = self.make(number, source, target, device)
        copy.start()
        self.sent.append(copy)

    def arrived(self, number, landed, device):
        self.make(number, landed, landed, device).wait_recv()

    def drain(self):
        for copy in self.sent:
            copy.wait_send()


def slot_match(experts, rows, per_expert):
    row = lax.broadcasted_iota(jnp.int32, (rows, TOK), 0)
    expert, half, slot = row // per_expert, (row // 4) % 2, row % 4
    one, zero = jnp.ones((rows, TOK), F32), jnp.zeros((rows, TOK), F32)
    first = jnp.where(jnp.broadcast_to(experts[0:1], (rows, TOK)) == expert, one, zero)
    second = jnp.where(jnp.broadcast_to(experts[1:2], (rows, TOK)) == expert, one, zero)
    left = lax.broadcasted_iota(jnp.int32, (TOK, TOK), 0)
    right = lax.broadcasted_iota(jnp.int32, (TOK, TOK), 1)
    earlier = jnp.where(left < right, 1.0, 0.0).astype(F32)
    before = dot(first + second, earlier, 1, 0)
    at_slot = jnp.where(before == slot.astype(F32), one, zero)
    upper = jnp.where(half == 0, one, zero)
    return first * at_slot, second * at_slot, upper


def selection(wanted):
    column = lax.broadcasted_iota(jnp.int32, (128, 128), 1)
    return jnp.where(column == wanted, 1.0, 0.0).astype(BF)


class Gather:
    def __init__(self, wire, ref, base, place, swap, ring, sibling):
        self.wire, self.ref, self.base, self.swap, self.sibling = wire, ref, base, swap, sibling
        self.x, self.core, self.y = place
        self.up, self.down, self.fore, self.back = ring

    def at(self, a, b, ci, start=0, count=ROWS):
        dx, dy = (b, a) if self.swap else (a, b)
        xi, yi = wrap(self.x + dx, NX), wrap(self.y + dy, NY)
        return self.ref.at[
            pl.ds(pl.multiple_of(yi * ROWS + start, 32), count),
            pl.ds(pl.multiple_of((xi * 2 + ci) * FEAT, 128), FEAT),
        ]

    def push(self, number, piece, device):
        self.wire.send(self.base + number, piece, piece, device)

    def got(self, number, piece):
        self.wire.arrived(self.base + number, piece, self.sibling)

    def start(self):
        own = self.at(0, 0, self.core)
        self.push(0, own, self.up)
        self.push(1, own, self.down)

    def spread(self, k, a):
        own = self.at(a, 0, self.core)
        self.push(4 + 4 * k, own, self.fore)
        self.push(5 + 4 * k, own, self.back)
        self.push(20 + 4 * k, own, self.sibling)

    def first_near(self):
        self.got(0, self.at(-1, 0, self.core))
        self.push(2, self.at(-1, 0, self.core, 0, 32), self.up)
        self.spread(1, -1)
        self.got(1, self.at(1, 0, self.core))
        self.push(3, self.at(1, 0, self.core, 32, 32), self.down)
        self.spread(2, 1)

    def first_far(self):
        self.got(2, self.at(2, 0, self.core, 0, 32))
        self.got(3, self.at(2, 0, self.core, 32, 32))
        self.spread(3, 2)

    def second_near(self, k, a):
        self.got(4 + 4 * k, self.at(a, -1, self.core))
        self.push(6 + 4 * k, self.at(a, -1, self.core, 0, 32), self.fore)
        self.push(21 + 4 * k, self.at(a, -1, self.core), self.sibling)
        self.got(5 + 4 * k, self.at(a, 1, self.core))
        self.push(7 + 4 * k, self.at(a, 1, self.core, 32, 32), self.back)
        self.push(22 + 4 * k, self.at(a, 1, self.core), self.sibling)

    def second_far(self, k, a):
        self.got(6 + 4 * k, self.at(a, 2, self.core, 0, 32))
        self.got(7 + 4 * k, self.at(a, 2, self.core, 32, 32))
        self.push(23 + 4 * k, self.at(a, 2, self.core), self.sibling)

    def from_sibling(self):
        for k, a in enumerate((0, -1, 1, 2)):
            for m, b in enumerate((0, -1, 1, 2)):
                self.got(20 + 4 * k + m, self.at(a, b, 1 - self.core))


class Scatter:
    def __init__(self, wire, base, buffers, a, b, first_peers, second_peers):
        self.wire, self.base = wire, base
        self.acc, self.near, self.full, self.mid, self.last = buffers
        self.a, self.b = a, b
        self.first_peers, self.second_peers = first_peers, second_peers

    def far(self):
        far = wrap(self.a + 2, 4)
        for side, peer in ((0, 0), (1, 2)):
            self.wire.send(
                self.base + side,
                self.acc.at[far, pl.ds(2 * side, 2)],
                self.near.at[side],
                self.first_peers[peer],
            )

    def close(self):
        for side, chunk, peer in ((0, 1, 0), (1, 3, 2)):
            self.wire.arrived(self.base + side, self.near.at[side], self.first_peers[peer])
            there = wrap(self.a + chunk, 4)
            for i in range(2):
                self.acc[there, 2 * side + i] = (
                    self.acc[there, 2 * side + i].astype(F32) + self.near[side, i].astype(F32)
                ).astype(BF)
            self.wire.send(
                self.base + 2 + side,
                self.acc.at[there],
                self.full.at[side],
                self.first_peers[peer],
            )

    def across(self):
        for side in range(2):
            self.wire.arrived(self.base + 2 + side, self.full.at[side], self.first_peers[0])
        for i in range(4):
            self.mid[i] = (
                self.acc[self.a, i].astype(F32)
                + self.full[0, i].astype(F32)
                + self.full[1, i].astype(F32)
            ).astype(BF)
        for d in range(1, 4):
            self.wire.send(
                self.base + 3 + d,
                self.mid.at[wrap(self.b + d, 4)],
                self.last.at[d - 1],
                self.second_peers[d - 1],
            )

    def total(self):
        result = self.mid[self.b].astype(F32)
        for d in range(1, 4):
            self.wire.arrived(self.base + 3 + d, self.last.at[d - 1], self.second_peers[0])
            result = result + self.last[d - 1].astype(F32)
        return result


def layer_kernel(
    tokens_hbm,
    cotangent_hbm,
    gates_hbm,
    experts_hbm,
    wg_hbm,
    wu_hbm,
    wd_hbm,
    grad_ref,
    routing_ref,
    dwg_hbm,
    dwu_hbm,
    dwd_hbm,
    tokens_ref,
    cotangent_ref,
    gates_ref,
    experts_ref,
    wg_ref,
    wu_ref,
    wd_ref,
    dwg_ref,
    dwu_ref,
    dwd_ref,
    load_sem,
    out_buf,
    in_buf,
    x_ref,
    c_ref,
    sums,
    gg_ref,
    gu_ref,
    hid_ref,
    r_out,
    r_in,
    acc_p,
    acc_q,
    near_p,
    near_q,
    full_p,
    full_q,
    mid_p,
    mid_q,
    last_p,
    last_q,
    t_ref,
    t_y,
    t_sum,
    t_t,
    back_out,
    back_in,
    send_sem,
    recv_sem,
):
    x, core, z, y = position()
    tensor = x * 2 + core
    small = [
        pltpu.make_async_copy(source, target, load_sem.at[i])
        for i, (source, target) in enumerate(
            (
                (experts_hbm, experts_ref),
                (gates_hbm, gates_ref),
                (tokens_hbm, tokens_ref),
                (cotangent_hbm, cotangent_ref),
            )
        )
    ]
    weights = [
        pltpu.make_async_copy(source, target, load_sem.at[4 + i])
        for i, (source, target) in enumerate(
            ((wg_hbm, wg_ref), (wu_hbm, wu_ref), (wd_hbm, wd_ref))
        )
    ]
    for copy in small:
        copy.start()
    peers_z = [device_of(x, core, wrap(z + d, NZ), y) for d in range(1, NZ)]
    peers_t = [{"tensor": wrap(tensor + d, 8), "wide": z * NY + y} for d in range(1, 8)]
    peers_y = [device_of(x, core, z, wrap(y + d, NY)) for d in range(1, NY)]
    peers_x = [device_of(wrap(x + d, NX), core, z, y) for d in range(1, NX)]
    sibling = device_of(x, 1 - core, z, y)

    barrier = pltpu.get_barrier_semaphore()
    partners = [peers_z[d - 1] for d in Z_ORDER] + peers_y + peers_t
    for partner in partners:
        pl.semaphore_signal(barrier, inc=1, device_id=partner, device_id_type=MESH)
    for copy in weights:
        copy.start()
    for copy in small:
        copy.wait()

    first, second, upper = slot_match(experts_ref[...], 64, 8)
    gates = gates_ref[...].astype(F32)
    pick_in = ((first + second) * upper).astype(BF)
    pick_up = ((first * gates[0:1] + second * gates[1:2]) * (1.0 - upper)).astype(BF)
    chosen = dot(pick_in, tokens_ref[...], 1, 0) + dot(pick_up, cotangent_ref[...], 1, 0)
    out_buf[...] = chosen.reshape(8, 8, FEAT).astype(BF)
    pl.semaphore_wait(barrier, len(partners))

    wire = Wire(send_sem, recv_sem)
    for d in Z_ORDER:
        there = wrap(z + d, NZ)
        wire.send(d - 1, out_buf.at[lax.div(there, 2)], in_buf.at[z], peers_z[d - 1])
    in_buf[z] = out_buf[lax.div(z, 2)]
    for d in Z_ORDER[::-1]:
        wire.arrived(d - 1, in_buf.at[wrap(z - d, NZ)], sibling)

    out_row = lax.broadcasted_iota(jnp.int32, (128, 128), 0)
    order = selection((out_row % 64) // 4 * 8 + out_row // 64 * 4 + out_row % 4)
    came = in_buf[...].astype(F32).reshape(128, FEAT).astype(BF)
    arranged = dot(order, came, 1, 0).astype(BF)
    my_rows = pl.ds(pl.multiple_of(y * ROWS, ROWS), ROWS)
    my_columns = pl.ds(pl.multiple_of(tensor * FEAT, 128), FEAT)
    x_ref[my_rows, my_columns] = arranged[0:64]
    c_ref[my_rows, my_columns] = arranged[64:128]

    on_x, on_y = [peers_x[0], peers_x[2]], [peers_y[0], peers_y[2]]
    place = (x, core, y)
    gathers = (
        Gather(wire, x_ref, 15, place, False, on_x + on_y, sibling),
        Gather(wire, c_ref, 51, place, True, on_y + on_x, sibling),
    )
    for one in gathers:
        one.start()
    for one in gathers:
        one.spread(0, 0)
    for one in gathers:
        one.first_near()
    for one in gathers:
        one.second_near(0, 0)
    for one in gathers:
        one.first_far()
    for k, a in ((1, -1), (2, 1)):
        for one in gathers:
            one.second_near(k, a)
        for one in gathers:
            one.second_far(k - 1, (0, -1)[k - 1])
    for one in gathers:
        one.second_near(3, 2)
    for one in gathers:
        one.second_far(2, 1)
    for one in gathers:
        one.second_far(3, 2)

    def columns_of(xi, ci):
        return pl.ds(pl.multiple_of((xi * 2 + ci) * FEAT, 128), FEAT)

    def forward(ci):
        gate = up = through = None
        for xi in range(NX):
            columns = columns_of(xi, ci)
            terms = (
                dot(x_ref[:, columns], wg_ref[0, columns, :], 1, 0),
                dot(x_ref[:, columns], wu_ref[0, columns, :], 1, 0),
                dot(c_ref[:, columns], wd_ref[0, :, columns], 1, 1),
            )
            if gate is None:
                gate, up, through = terms
            else:
                gate, up, through = gate + terms[0], up + terms[1], through + terms[2]
        return gate, up, through

    for copy in weights:
        copy.wait()
    sums[0], sums[1], sums[2] = forward(core)
    for one in gathers:
        one.from_sibling()
    pre_gate, pre_up, hidden_grad = forward(1 - core)
    pre_gate, pre_up, hidden_grad = pre_gate + sums[0], pre_up + sums[1], hidden_grad + sums[2]
    sig = jax.nn.sigmoid(pre_gate)
    act = pre_gate * sig
    hidden = act * pre_up
    gg_ref[...] = (hidden_grad * pre_up * sig * (1.0 + pre_gate * (1.0 - sig))).astype(BF)
    gu_ref[...] = (hidden_grad * act).astype(BF)
    hid_ref[...] = hidden.astype(BF)
    row = lax.broadcasted_iota(jnp.int32, (ROWS, 128), 0)
    lane = lax.broadcasted_iota(jnp.int32, (ROWS, 128), 1)
    row_sums = jnp.sum(hidden_grad * hidden, axis=1, keepdims=True)
    for yi in range(NY):
        part = jnp.broadcast_to(row_sums[yi * ROWS : (yi + 1) * ROWS], (ROWS, 128))
        line = jnp.sum(jnp.where(row == lane, part, 0.0), axis=0, keepdims=True)
        t_ref[yi] = jnp.broadcast_to(line, (8, 128))
    for d in range(1, NY):
        wire.send(86 + d, t_ref.at[wrap(y + d, NY)], t_y.at[d - 1], peers_y[d - 1])

    def returned(xi, ci):
        columns = columns_of(xi, ci)
        return dot(gg_ref[...], wg_ref[0, columns, :], 1, 1) + dot(
            gu_ref[...], wu_ref[0, columns, :], 1, 1
        )

    x_order = (2, 1, 3, 0)
    for k, d in enumerate(x_order):
        r_out[k] = returned(wrap(x + d, NX), 1 - core).astype(BF)
        wire.send(90 + k, r_out.at[k], r_in.at[k], sibling)
    for k, d in enumerate(x_order):
        xi = wrap(x + d, NX)
        own = returned(xi, core)
        wire.arrived(90 + k, r_in.at[k], sibling)
        total = (own + r_in[k].astype(F32)).astype(BF)
        for yi in range(NY):
            acc_p[xi, yi] = total[yi * ROWS : yi * ROWS + 32]
            acc_q[yi, xi] = total[yi * ROWS + 32 : yi * ROWS + 64]

    def weight_grads(which):
        step = 512
        for k in range(D // step):
            rows = pl.ds(k * step, step)
            if which == 0:
                dwd_ref[0, :, rows] = dot(hid_ref[...], c_ref[:, rows], 0, 0).astype(BF)
            if which == 1:
                dwg_ref[0, rows, :] = dot(x_ref[:, rows], gg_ref[...], 0, 0).astype(BF)
            if which == 2:
                dwu_ref[0, rows, :] = dot(x_ref[:, rows], gu_ref[...], 0, 0).astype(BF)

    stores = [
        pltpu.make_async_copy(source, target, load_sem.at[7 + i])
        for i, (source, target) in enumerate(
            ((dwd_ref, dwd_hbm), (dwg_ref, dwg_hbm), (dwu_ref, dwu_hbm))
        )
    ]
    scatters = (
        Scatter(
            wire, 94, (acc_p, near_p, full_p, mid_p, last_p), x, y, peers_x, peers_y
        ),
        Scatter(
            wire, 101, (acc_q, near_q, full_q, mid_q, last_q), y, x, peers_y, peers_x
        ),
    )
    for one in scatters:
        one.far()
    line = t_ref[y]
    for d in range(1, NY):
        wire.arrived(86 + d, t_y.at[d - 1], sibling)
        line = line + t_y[d - 1]
    t_sum[...] = line
    t_t[tensor] = line
    for d in range(1, 8):
        wire.send(107 + d, t_sum, t_t.at[tensor], peers_t[d - 1])
    weight_grads(0)
    stores[0].start()
    for one in scatters:
        one.close()
    weight_grads(1)
    stores[1].start()
    for one in scatters:
        one.across()
    for d in range(1, 8):
        wire.arrived(107 + d, t_t.at[wrap(tensor - d, 8)], sibling)
    line = t_t[0]
    for i in range(1, 8):
        line = line + t_t[i]
    spread = jnp.where(row == lane, jnp.broadcast_to(line[0:1], (ROWS, 128)), 0.0)
    column = jnp.broadcast_to(jnp.sum(spread, axis=1, keepdims=True), (ROWS, 128))
    result = jnp.concatenate([one.total() for one in scatters], axis=0)
    pair = jnp.concatenate(
        [
            result[:, 0:256],
            jnp.concatenate([result[:, 256:FEAT], column], axis=1),
        ],
        axis=0,
    ).astype(BF)
    order = selection((out_row // 4) % 2 * 64 + out_row // 8 * 4 + out_row % 4)
    back_out[...] = dot(order, pair, 1, 0).reshape(NZ, 8, 256).astype(BF)
    for d in Z_ORDER:
        wire.send(114 + d, back_out.at[wrap(z + d, NZ)], back_in.at[z], peers_z[d - 1])
    back_in[z] = back_out[z]
    weight_grads(2)
    stores[2].start()

    first, second, upper = slot_match(experts_ref[...], 128, 16)
    lower = 1.0 - upper
    pick_head = ((first + second) * upper).astype(BF)
    pick_tail = ((first + second) * lower).astype(BF)
    pick_first = (first * lower).astype(BF)
    pick_second = (second * lower).astype(BF)
    for d in Z_ORDER[::-1]:
        wire.arrived(114 + d, back_in.at[wrap(z - d, NZ)], sibling)
    came = back_in[...].astype(F32).reshape(128, 256).astype(BF)
    grad_ref[:, 0:256] = dot(pick_head, came, 0, 0).astype(BF)
    grad_ref[:, 256:FEAT] = dot(pick_tail, came[:, 0:128], 0, 0).astype(BF)
    at_first = dot(came[:, 128:], pick_first, 0, 0)
    at_second = dot(came[:, 128:], pick_second, 0, 0)
    routing_ref[0:1, :] = at_first[0:1, :] / gates[0:1]
    routing_ref[1:2, :] = at_second[0:1, :] / gates[1:2]
    for copy in stores:
        copy.wait()
    wire.drain()


def layer(*arguments):
    quarter = [pltpu.VMEM((4, 4, 32, FEAT), BF)] * 2
    near = [pltpu.VMEM((2, 2, 32, FEAT), BF)] * 2
    full = [pltpu.VMEM((2, 4, 32, FEAT), BF)] * 2
    mid = [pltpu.VMEM((4, 32, FEAT), BF)] * 2
    last = [pltpu.VMEM((3, 32, FEAT), BF)] * 2
    return pl.pallas_call(
        layer_kernel,
        name="layer",
        out_shape=(
            jax.ShapeDtypeStruct((TOK, FEAT), BF),
            jax.ShapeDtypeStruct((2, TOK), F32),
            jax.ShapeDtypeStruct((1, D, HID), BF),
            jax.ShapeDtypeStruct((1, D, HID), BF),
            jax.ShapeDtypeStruct((1, HID, D), BF),
        ),
        in_specs=[HBM] * 7,
        out_specs=(VMEM, VMEM, HBM, HBM, HBM),
        scratch_shapes=[
            pltpu.VMEM((TOK, FEAT), BF),
            pltpu.VMEM((TOK, FEAT), BF),
            pltpu.VMEM((2, TOK), BF),
            pltpu.VMEM((2, TOK), jnp.int32),
            pltpu.VMEM((1, D, HID), BF),
            pltpu.VMEM((1, D, HID), BF),
            pltpu.VMEM((1, HID, D), BF),
            pltpu.VMEM((1, D, HID), BF),
            pltpu.VMEM((1, D, HID), BF),
            pltpu.VMEM((1, HID, D), BF),
            pltpu.SemaphoreType.DMA((10,)),
            pltpu.VMEM((8, 8, FEAT), BF),
            pltpu.VMEM((NZ, 8, FEAT), BF),
            pltpu.VMEM((SLOTS, D), BF),
            pltpu.VMEM((SLOTS, D), BF),
            pltpu.VMEM((3, SLOTS, HID), F32),
            pltpu.VMEM((SLOTS, HID), BF),
            pltpu.VMEM((SLOTS, HID), BF),
            pltpu.VMEM((SLOTS, HID), BF),
            pltpu.VMEM((NX, SLOTS, FEAT), BF),
            pltpu.VMEM((NX, SLOTS, FEAT), BF),
            *quarter,
            *near,
            *full,
            *mid,
            *last,
            pltpu.VMEM((NY, 8, 128), F32),
            pltpu.VMEM((3, 8, 128), F32),
            pltpu.VMEM((8, 128), F32),
            pltpu.VMEM((8, 8, 128), F32),
            pltpu.VMEM((NZ, 8, 256), BF),
            pltpu.VMEM((NZ, 8, 256), BF),
            pltpu.SemaphoreType.DMA((130,)),
            pltpu.SemaphoreType.DMA((130,)),
        ],
        compiler_params=pltpu.CompilerParams(
            collective_id=0, has_side_effects=True, vmem_limit_bytes=60 << 20
        ),
    )(*arguments)


def emit_kernel(*refs):
    sources, targets, stage, load_sem, store_sem = refs[:5], refs[5:10], refs[10:15], refs[15], refs[16]
    pieces = [(i, None) for i in range(2)]
    pieces += [(i, part) for part in range(2) for i in range(2, 5)]

    def view(ref, part):
        if part is None:
            return ref
        half = ref.shape[1] // 2
        return ref.at[:, pl.ds(part * half, half)]

    loads = [
        pltpu.make_async_copy(view(sources[i], part), view(stage[i], part), load_sem.at[n])
        for n, (i, part) in enumerate(pieces)
    ]
    stores = [
        pltpu.make_async_copy(view(stage[i], part), view(targets[i], part), store_sem.at[n])
        for n, (i, part) in enumerate(pieces)
    ]
    for copy in loads:
        copy.start()
    for load, store in zip(loads, stores):
        load.wait()
        store.start()
    for copy in stores:
        copy.wait()


def emit(*results):
    return pl.pallas_call(
        emit_kernel,
        name="emit",
        out_shape=tuple(jax.ShapeDtypeStruct(one.shape, one.dtype) for one in results),
        in_specs=[HBM] * 5,
        out_specs=(HBM,) * 5,
        scratch_shapes=[
            *[pltpu.VMEM(one.shape, one.dtype) for one in results],
            pltpu.SemaphoreType.DMA((8,)),
            pltpu.SemaphoreType.DMA((8,)),
        ],
        compiler_params=pltpu.CompilerParams(vmem_limit_bytes=60 << 20),
    )(*results)


def shards(tokens, cotangent, gates, experts, w_gate, w_up, w_down):
    results = layer(tokens, cotangent, gates.T, experts.T, w_gate, w_up, w_down)
    input_grad, routing_grad, gate_grad, up_grad, down_grad = emit(*results)
    return input_grad, routing_grad.T, gate_grad, up_grad, down_grad


def solution(mesh):
    return jax.shard_map(
        shards,
        mesh=mesh,
        in_specs=(
            P("wide", "tensor"),
            P("wide", "tensor"),
            P("wide", None),
            P("wide", None),
            P("wide", None, "tensor"),
            P("wide", None, "tensor"),
            P("wide", "tensor", None),
        ),
        out_specs=(
            P("wide", "tensor"),
            P("wide", None),
            P("wide", None, "tensor"),
            P("wide", None, "tensor"),
            P("wide", "tensor", None),
        ),
        check_vma=False,
    )
```

time: 395 us -> 70.8 us (0.18)
  the two profiles are of different devices: /device:TPU:16 before, /device:TPU:4 now
where the time goes in v2:
time: 70.8 us; the launch traced here: 70.7 us
  Pallas kernels  70 us (99%)
    pallas_call x1, Pallas kernels, layer(): pl.pallas_call(layer_kernel, name='layer', out_shape=(jax.ShapeDtypeStruc...  67.5 us
    pallas_call x1, Pallas kernels, emit(): pl.pallas_call(emit_kernel, name='emit', out_shape=tuple((jax.ShapeDtypeS...  2.55 us

profile of v2, /device:TPU:4, one launch (start us, length us, event | category | flops | bytes accessed | tf_op | source)
XLA Modules:
  0.0 70.7 jit_solution(15425012859144965241)
XLA Ops:
  0.6 67.5 %layer.1 = (bf16[8,384]{1,0:T(8,128)(2,1)}, f32[2,8]{1,0:T(2,128)}, bf16[1,3072,128]{2,1,0:T(8,128)(2,1)}, bf16[1,3072,128]{2,1,0:T(8,128)(2,1)}, bf16[1,128,3072]{2,1,0:T(8,128)(2,1)}) custom-call(bf16[8,384]{1,0:T(8,128)(2,1)} %tokens_hbm.1, bf16[8,384]{1,0:T(8,128)(2,1)} %cotangent_hbm.1, bf16[2,8]{1,0:T(2,128)(2,1)} %bitcast.4, s32[2,8]{1,0:T(2,128)} %bitcast.3, ...), custom_call_target="tpu_custom_call" | custom-call | tf_op jit(solution)/shard_map/layer/pallas_call | solution.py:509
  68.1 2.5 %emit.1 = (bf16[8,384]{1,0:T(8,128)(2,1)}, f32[2,8]{1,0:T(2,128)}, bf16[1,3072,128]{2,1,0:T(8,128)(2,1)}, bf16[1,3072,128]{2,1,0:T(8,128)(2,1)}, bf16[1,128,3072]{2,1,0:T(8,128)(2,1)}) custom-call(bf16[8,384]{1,0:T(8,128)(2,1)} %get-tuple-element.15.refs_0_, f32[2,8]{1,0:T(2,128)} %get-tuple-element.16.refs_1_, ...), custom_call_target="tpu_custom_call" | custom-call | tf_op jit(solution)/shard_map/emit/pallas_call | solution.py:592

commit v3 on v2

--- a/solution.py
+++ b/solution.py
@@ -93,16 +93,16 @@
 
 
 class Gather:
-    def __init__(self, wire, ref, base, place, swap, ring, sibling):
+    def __init__(self, wire, ref, base, place, swap, first_peers, second_peers, sibling):
         self.wire, self.ref, self.base, self.swap, self.sibling = wire, ref, base, swap, sibling
         self.x, self.core, self.y = place
-        self.up, self.down, self.fore, self.back = ring
-
-    def at(self, a, b, ci, start=0, count=ROWS):
+        self.first_peers, self.second_peers = first_peers, second_peers
+
+    def at(self, a, b, ci):
         dx, dy = (b, a) if self.swap else (a, b)
-        xi, yi = wrap(self.x + dx, NX), wrap(self.y + dy, NY)
+        xi, yi = wrap(self.x - dx, NX), wrap(self.y - dy, NY)
         return self.ref.at[
-            pl.ds(pl.multiple_of(yi * ROWS + start, 32), count),
+            pl.ds(pl.multiple_of(yi * ROWS, ROWS), ROWS),
             pl.ds(pl.multiple_of((xi * 2 + ci) * FEAT, 128), FEAT),
         ]
 
@@ -113,101 +113,64 @@
         self.wire.arrived(self.base + number, piece, self.sibling)
 
     def start(self):
-        own = self.at(0, 0, self.core)
-        self.push(0, own, self.up)
-        self.push(1, own, self.down)
-
-    def spread(self, k, a):
-        own = self.at(a, 0, self.core)
-        self.push(4 + 4 * k, own, self.fore)
-        self.push(5 + 4 * k, own, self.back)
-        self.push(20 + 4 * k, own, self.sibling)
-
-    def first_near(self):
-        self.got(0, self.at(-1, 0, self.core))
-        self.push(2, self.at(-1, 0, self.core, 0, 32), self.up)
-        self.spread(1, -1)
-        self.got(1, self.at(1, 0, self.core))
-        self.push(3, self.at(1, 0, self.core, 32, 32), self.down)
-        self.spread(2, 1)
-
-    def first_far(self):
-        self.got(2, self.at(2, 0, self.core, 0, 32))
-        self.got(3, self.at(2, 0, self.core, 32, 32))
-        self.spread(3, 2)
-
-    def second_near(self, k, a):
-        self.got(4 + 4 * k, self.at(a, -1, self.core))
-        self.push(6 + 4 * k, self.at(a, -1, self.core, 0, 32), self.fore)
-        self.push(21 + 4 * k, self.at(a, -1, self.core), self.sibling)
-        self.got(5 + 4 * k, self.at(a, 1, self.core))
-        self.push(7 + 4 * k, self.at(a, 1, self.core, 32, 32), self.back)
-        self.push(22 + 4 * k, self.at(a, 1, self.core), self.sibling)
-
-    def second_far(self, k, a):
-        self.got(6 + 4 * k, self.at(a, 2, self.core, 0, 32))
-        self.got(7 + 4 * k, self.at(a, 2, self.core, 32, 32))
-        self.push(23 + 4 * k, self.at(a, 2, self.core), self.sibling)
+        for d in (2, 1, 3):
+            self.push(d - 1, self.at(0, 0, self.core), self.first_peers[d - 1])
+
+    def spread(self, k):
+        block = self.at(k, 0, self.core)
+        if k:
+            self.got(k - 1, block)
+        for d in (2, 1, 3):
+            self.push(3 * k + 2 + d, block, self.second_peers[d - 1])
+
+    def feed(self, k, m):
+        block = self.at(k, m, self.core)
+        if m:
+            self.got(3 * k + 2 + m, block)
+        self.push(15 + 4 * k + m, block, self.sibling)
 
     def from_sibling(self):
-        for k, a in enumerate((0, -1, 1, 2)):
-            for m, b in enumerate((0, -1, 1, 2)):
-                self.got(20 + 4 * k + m, self.at(a, b, 1 - self.core))
+        for k in range(4):
+            for m in range(4):
+                self.got(15 + 4 * k + m, self.at(k, m, 1 - self.core))
 
 
 class Scatter:
     def __init__(self, wire, base, buffers, a, b, first_peers, second_peers):
         self.wire, self.base = wire, base
-        self.acc, self.near, self.full, self.mid, self.last = buffers
+        self.acc, self.full, self.mid, self.last = buffers
         self.a, self.b = a, b
         self.first_peers, self.second_peers = first_peers, second_peers
 
-    def far(self):
-        far = wrap(self.a + 2, 4)
-        for side, peer in ((0, 0), (1, 2)):
-            self.wire.send(
-                self.base + side,
-                self.acc.at[far, pl.ds(2 * side, 2)],
-                self.near.at[side],
-                self.first_peers[peer],
-            )
-
-    def close(self):
-        for side, chunk, peer in ((0, 1, 0), (1, 3, 2)):
-            self.wire.arrived(self.base + side, self.near.at[side], self.first_peers[peer])
-            there = wrap(self.a + chunk, 4)
-            for i in range(2):
-                self.acc[there, 2 * side + i] = (
-                    self.acc[there, 2 * side + i].astype(F32) + self.near[side, i].astype(F32)
-                ).astype(BF)
-            self.wire.send(
-                self.base + 2 + side,
-                self.acc.at[there],
-                self.full.at[side],
-                self.first_peers[peer],
-            )
+    def send(self, d):
+        self.wire.send(
+            self.base + d - 1,
+            self.acc.at[wrap(self.a + d, 4)],
+            self.full.at[d - 1],
+            self.first_peers[d - 1],
+        )
 
     def across(self):
-        for side in range(2):
-            self.wire.arrived(self.base + 2 + side, self.full.at[side], self.first_peers[0])
-        for i in range(4):
-            self.mid[i] = (
-                self.acc[self.a, i].astype(F32)
-                + self.full[0, i].astype(F32)
-                + self.full[1, i].astype(F32)
-            ).astype(BF)
-        for d in range(1, 4):
-            self.wire.send(
-                self.base + 3 + d,
-                self.mid.at[wrap(self.b + d, 4)],
-                self.last.at[d - 1],
-                self.second_peers[d - 1],
-            )
+        for d in (1, 3, 2):
+            self.wire.arrived(self.base + d - 1, self.full.at[d - 1], self.first_peers[0])
+        for d in (2, 1, 3, 0):
+            i = wrap(self.b + d, 4)
+            total = self.acc[self.a, i].astype(F32)
+            for e in range(3):
+                total = total + self.full[e, i].astype(F32)
+            self.mid[i] = total.astype(BF)
+            if d:
+                self.wire.send(
+                    self.base + 2 + d,
+                    self.mid.at[i],
+                    self.last.at[d - 1],
+                    self.second_peers[d - 1],
+                )
 
     def total(self):
         result = self.mid[self.b].astype(F32)
         for d in range(1, 4):
-            self.wire.arrived(self.base + 3 + d, self.last.at[d - 1], self.second_peers[0])
+            self.wire.arrived(self.base + 2 + d, self.last.at[d - 1], self.second_peers[0])
             result = result + self.last[d - 1].astype(F32)
         return result
 
@@ -248,8 +211,6 @@
     r_in,
     acc_p,
     acc_q,
-    near_p,
-    near_q,
     full_p,
     full_q,
     mid_p,
@@ -326,33 +287,22 @@
     x_ref[my_rows, my_columns] = arranged[0:64]
     c_ref[my_rows, my_columns] = arranged[64:128]
 
-    on_x, on_y = [peers_x[0], peers_x[2]], [peers_y[0], peers_y[2]]
     place = (x, core, y)
     gathers = (
-        Gather(wire, x_ref, 15, place, False, on_x + on_y, sibling),
-        Gather(wire, c_ref, 51, place, True, on_y + on_x, sibling),
+        Gather(wire, x_ref, 15, place, False, peers_x, peers_y, sibling),
+        Gather(wire, c_ref, 46, place, True, peers_y, peers_x, sibling),
     )
     for one in gathers:
         one.start()
     for one in gathers:
-        one.spread(0, 0)
-    for one in gathers:
-        one.first_near()
-    for one in gathers:
-        one.second_near(0, 0)
-    for one in gathers:
-        one.first_far()
-    for k, a in ((1, -1), (2, 1)):
+        one.spread(0)
+    for k in (1, 3, 2):
         for one in gathers:
-            one.second_near(k, a)
-        for one in gathers:
-            one.second_far(k - 1, (0, -1)[k - 1])
-    for one in gathers:
-        one.second_near(3, 2)
-    for one in gathers:
-        one.second_far(2, 1)
-    for one in gathers:
-        one.second_far(3, 2)
+            one.spread(k)
+    for k in (0, 1, 3, 2):
+        for m in (0, 1, 3, 2):
+            for one in gathers:
+                one.feed(k, m)
 
     def columns_of(xi, ci):
         return pl.ds(pl.multiple_of((xi * 2 + ci) * FEAT, 128), FEAT)
@@ -384,6 +334,21 @@
     hidden = act * pre_up
     gg_ref[...] = (hidden_grad * pre_up * sig * (1.0 + pre_gate * (1.0 - sig))).astype(BF)
     gu_ref[...] = (hidden_grad * act).astype(BF)
+
+    def returned(xi, ci):
+        columns = columns_of(xi, ci)
+        return dot(gg_ref[...], wg_ref[0, columns, :], 1, 1) + dot(
+            gu_ref[...], wu_ref[0, columns, :], 1, 1
+        )
+
+    scatters = (
+        Scatter(wire, 94, (acc_p, full_p, mid_p, last_p), x, y, peers_x, peers_y),
+        Scatter(wire, 101, (acc_q, full_q, mid_q, last_q), y, x, peers_y, peers_x),
+    )
+    x_order = (2, 1, 3, 0)
+    for k, d in enumerate(x_order):
+        r_out[k] = returned(wrap(x + d, NX), 1 - core).astype(BF)
+        wire.send(90 + k, r_out.at[k], r_in.at[k], sibling)
     hid_ref[...] = hidden.astype(BF)
     row = lax.broadcasted_iota(jnp.int32, (ROWS, 128), 0)
     lane = lax.broadcasted_iota(jnp.int32, (ROWS, 128), 1)
@@ -394,17 +359,6 @@
         t_ref[yi] = jnp.broadcast_to(line, (8, 128))
     for d in range(1, NY):
         wire.send(86 + d, t_ref.at[wrap(y + d, NY)], t_y.at[d - 1], peers_y[d - 1])
-
-    def returned(xi, ci):
-        columns = columns_of(xi, ci)
-        return dot(gg_ref[...], wg_ref[0, columns, :], 1, 1) + dot(
-            gu_ref[...], wu_ref[0, columns, :], 1, 1
-        )
-
-    x_order = (2, 1, 3, 0)
-    for k, d in enumerate(x_order):
-        r_out[k] = returned(wrap(x + d, NX), 1 - core).astype(BF)
-        wire.send(90 + k, r_out.at[k], r_in.at[k], sibling)
     for k, d in enumerate(x_order):
         xi = wrap(x + d, NX)
         own = returned(xi, core)
@@ -413,6 +367,10 @@
         for yi in range(NY):
             acc_p[xi, yi] = total[yi * ROWS : yi * ROWS + 32]
             acc_q[yi, xi] = total[yi * ROWS + 32 : yi * ROWS + 64]
+        if d:
+            scatters[0].send(d)
+    for d in (2, 1, 3):
+        scatters[1].send(d)
 
     def weight_grads(which):
         step = 512
@@ -431,16 +389,6 @@
             ((dwd_ref, dwd_hbm), (dwg_ref, dwg_hbm), (dwu_ref, dwu_hbm))
         )
     ]
-    scatters = (
-        Scatter(
-            wire, 94, (acc_p, near_p, full_p, mid_p, last_p), x, y, peers_x, peers_y
-        ),
-        Scatter(
-            wire, 101, (acc_q, near_q, full_q, mid_q, last_q), y, x, peers_y, peers_x
-        ),
-    )
-    for one in scatters:
-        one.far()
     line = t_ref[y]
     for d in range(1, NY):
         wire.arrived(86 + d, t_y.at[d - 1], sibling)
@@ -451,12 +399,12 @@
         wire.send(107 + d, t_sum, t_t.at[tensor], peers_t[d - 1])
     weight_grads(0)
     stores[0].start()
-    for one in scatters:
-        one.close()
     weight_grads(1)
     stores[1].start()
     for one in scatters:
         one.across()
+    weight_grads(2)
+    stores[2].start()
     for d in range(1, 8):
         wire.arrived(107 + d, t_t.at[wrap(tensor - d, 8)], sibling)
     line = t_t[0]
@@ -477,8 +425,6 @@
     for d in Z_ORDER:
         wire.send(114 + d, back_out.at[wrap(z + d, NZ)], back_in.at[z], peers_z[d - 1])
     back_in[z] = back_out[z]
-    weight_grads(2)
-    stores[2].start()
 
     first, second, upper = slot_match(experts_ref[...], 128, 16)
     lower = 1.0 - upper
@@ -502,8 +448,7 @@
 
 def layer(*arguments):
     quarter = [pltpu.VMEM((4, 4, 32, FEAT), BF)] * 2
-    near = [pltpu.VMEM((2, 2, 32, FEAT), BF)] * 2
-    full = [pltpu.VMEM((2, 4, 32, FEAT), BF)] * 2
+    full = [pltpu.VMEM((3, 4, 32, FEAT), BF)] * 2
     mid = [pltpu.VMEM((4, 32, FEAT), BF)] * 2
     last = [pltpu.VMEM((3, 32, FEAT), BF)] * 2
     return pl.pallas_call(
@@ -541,7 +486,6 @@
             pltpu.VMEM((NX, SLOTS, FEAT), BF),
             pltpu.VMEM((NX, SLOTS, FEAT), BF),
             *quarter,
-            *near,
             *full,
             *mid,
             *last,

time: 70.8 us -> 64.5 us (0.911)
  the two profiles are of different devices: /device:TPU:4 before, /device:TPU:8 now
where the time goes in v3:
time: 64.5 us; the launch traced here: 64.4 us
  Pallas kernels  63.7 us (99%)
    pallas_call x1, Pallas kernels, layer(): pl.pallas_call(layer_kernel, name='layer', out_shape=(jax.ShapeDtypeStruc...  61.2 us
    pallas_call x1, Pallas kernels, emit(): pl.pallas_call(emit_kernel, name='emit', out_shape=tuple((jax.ShapeDtypeS...  2.55 us

profile of v3, /device:TPU:8, one launch (start us, length us, event | category | flops | bytes accessed | tf_op | source)
XLA Modules:
  0.0 64.4 jit_solution(14969619859028408493)
XLA Ops:
  0.6 61.2 %layer.1 = (bf16[8,384]{1,0:T(8,128)(2,1)}, f32[2,8]{1,0:T(2,128)}, bf16[1,3072,128]{2,1,0:T(8,128)(2,1)}, bf16[1,3072,128]{2,1,0:T(8,128)(2,1)}, bf16[1,128,3072]{2,1,0:T(8,128)(2,1)}) custom-call(bf16[8,384]{1,0:T(8,128)(2,1)} %tokens_hbm.1, bf16[8,384]{1,0:T(8,128)(2,1)} %cotangent_hbm.1, bf16[2,8]{1,0:T(2,128)(2,1)} %bitcast.4, s32[2,8]{1,0:T(2,128)} %bitcast.3, ...), custom_call_target="tpu_custom_call" | custom-call | tf_op jit(solution)/shard_map/layer/pallas_call | solution.py:454
  61.8 2.5 %emit.1 = (bf16[8,384]{1,0:T(8,128)(2,1)}, f32[2,8]{1,0:T(2,128)}, bf16[1,3072,128]{2,1,0:T(8,128)(2,1)}, bf16[1,3072,128]{2,1,0:T(8,128)(2,1)}, bf16[1,128,3072]{2,1,0:T(8,128)(2,1)}) custom-call(bf16[8,384]{1,0:T(8,128)(2,1)} %get-tuple-element.15.refs_0_, f32[2,8]{1,0:T(2,128)} %get-tuple-element.16.refs_1_, ...), custom_call_target="tpu_custom_call" | custom-call | tf_op jit(solution)/shard_map/emit/pallas_call | solution.py:536

commit v4 on v3

--- a/solution.py
+++ b/solution.py
@@ -70,6 +70,7 @@
     def drain(self):
         for copy in self.sent:
             copy.wait_send()
+        self.sent = []
 
 
 def slot_match(experts, rows, per_expert):
@@ -150,9 +151,27 @@
             self.first_peers[d - 1],
         )
 
-    def across(self):
+    def send_piece(self, k, i):
+        for d in (2, 1, 3):
+            self.wire.send(
+                self.base + 6 + 3 * k + d - 1,
+                self.acc.at[wrap(self.a + d, 4), i],
+                self.full.at[d - 1, i],
+                self.first_peers[d - 1],
+            )
+
+    def pieces(self, order):
+        for k, i in enumerate(order):
+            for d in (1, 3, 2):
+                self.wire.arrived(
+                    self.base + 6 + 3 * k + d - 1, self.full.at[d - 1, i], self.first_peers[0]
+                )
+
+    def chunks(self):
         for d in (1, 3, 2):
             self.wire.arrived(self.base + d - 1, self.full.at[d - 1], self.first_peers[0])
+
+    def across(self):
         for d in (2, 1, 3, 0):
             i = wrap(self.b + d, 4)
             total = self.acc[self.a, i].astype(F32)
@@ -183,11 +202,13 @@
     wg_hbm,
     wu_hbm,
     wd_hbm,
-    grad_ref,
-    routing_ref,
+    grad_hbm,
+    routing_hbm,
     dwg_hbm,
     dwu_hbm,
     dwd_hbm,
+    grad_ref,
+    routing_ref,
     tokens_ref,
     cotangent_ref,
     gates_ref,
@@ -343,7 +364,7 @@
 
     scatters = (
         Scatter(wire, 94, (acc_p, full_p, mid_p, last_p), x, y, peers_x, peers_y),
-        Scatter(wire, 101, (acc_q, full_q, mid_q, last_q), y, x, peers_y, peers_x),
+        Scatter(wire, 130, (acc_q, full_q, mid_q, last_q), y, x, peers_y, peers_x),
     )
     x_order = (2, 1, 3, 0)
     for k, d in enumerate(x_order):
@@ -369,8 +390,7 @@
             acc_q[yi, xi] = total[yi * ROWS + 32 : yi * ROWS + 64]
         if d:
             scatters[0].send(d)
-    for d in (2, 1, 3):
-        scatters[1].send(d)
+        scatters[1].send_piece(k, xi)
 
     def weight_grads(which):
         step = 512
@@ -401,8 +421,10 @@
     stores[0].start()
     weight_grads(1)
     stores[1].start()
-    for one in scatters:
-        one.across()
+    scatters[1].pieces([wrap(x + d, NX) for d in x_order])
+    scatters[1].across()
+    scatters[0].chunks()
+    scatters[0].across()
     weight_grads(2)
     stores[2].start()
     for d in range(1, 8):
@@ -422,6 +444,8 @@
     ).astype(BF)
     order = selection((out_row // 4) % 2 * 64 + out_row // 8 * 4 + out_row % 4)
     back_out[...] = dot(order, pair, 1, 0).reshape(NZ, 8, 256).astype(BF)
+    earlier = Wire(send_sem, recv_sem)
+    earlier.sent, wire.sent = wire.sent, []
     for d in Z_ORDER:
         wire.send(114 + d, back_out.at[wrap(z + d, NZ)], back_in.at[z], peers_z[d - 1])
     back_in[z] = back_out[z]
@@ -432,18 +456,27 @@
     pick_tail = ((first + second) * lower).astype(BF)
     pick_first = (first * lower).astype(BF)
     pick_second = (second * lower).astype(BF)
+    earlier.drain()
+    for copy in stores:
+        copy.wait()
     for d in Z_ORDER[::-1]:
         wire.arrived(114 + d, back_in.at[wrap(z - d, NZ)], sibling)
     came = back_in[...].astype(F32).reshape(128, 256).astype(BF)
     grad_ref[:, 0:256] = dot(pick_head, came, 0, 0).astype(BF)
     grad_ref[:, 256:FEAT] = dot(pick_tail, came[:, 0:128], 0, 0).astype(BF)
+    results = [
+        pltpu.make_async_copy(grad_ref, grad_hbm, load_sem.at[0]),
+        pltpu.make_async_copy(routing_ref, routing_hbm, load_sem.at[1]),
+    ]
+    results[0].start()
     at_first = dot(came[:, 128:], pick_first, 0, 0)
     at_second = dot(came[:, 128:], pick_second, 0, 0)
     routing_ref[0:1, :] = at_first[0:1, :] / gates[0:1]
     routing_ref[1:2, :] = at_second[0:1, :] / gates[1:2]
-    for copy in stores:
+    results[1].start()
+    wire.drain()
+    for copy in results:
         copy.wait()
-    wire.drain()
 
 
 def layer(*arguments):
@@ -462,8 +495,10 @@
             jax.ShapeDtypeStruct((1, HID, D), BF),
         ),
         in_specs=[HBM] * 7,
-        out_specs=(VMEM, VMEM, HBM, HBM, HBM),
+        out_specs=(HBM,) * 5,
         scratch_shapes=[
+            pltpu.VMEM((TOK, FEAT), BF),
+            pltpu.VMEM((2, TOK), F32),
             pltpu.VMEM((TOK, FEAT), BF),
             pltpu.VMEM((TOK, FEAT), BF),
             pltpu.VMEM((2, TOK), BF),
@@ -495,8 +530,8 @@
             pltpu.VMEM((8, 8, 128), F32),
             pltpu.VMEM((NZ, 8, 256), BF),
             pltpu.VMEM((NZ, 8, 256), BF),
-            pltpu.SemaphoreType.DMA((130,)),
-            pltpu.SemaphoreType.DMA((130,)),
+            pltpu.SemaphoreType.DMA((148,)),
+            pltpu.SemaphoreType.DMA((148,)),
         ],
         compiler_params=pltpu.CompilerParams(
             collective_id=0, has_side_effects=True, vmem_limit_bytes=60 << 20

time: 64.5 us -> 63.9 us (level)
  the two profiles are of different devices: /device:TPU:8 before, /device:TPU:2 now
where the time goes in v4:
time: 63.9 us; the launch traced here: 63.7 us
  Pallas kernels  63.1 us (99%)
  between operations  0.64 us (1%)
    pallas_call x1, Pallas kernels, layer(): pl.pallas_call(layer_kernel, name='layer', out_shape=(jax.ShapeDtypeStruc...  60.5 us
    pallas_call x1, Pallas kernels, emit(): pl.pallas_call(emit_kernel, name='emit', out_shape=tuple((jax.ShapeDtypeS...  2.55 us

profile of v4, /device:TPU:2, one launch (start us, length us, event | category | flops | bytes accessed | tf_op | source)
XLA Modules:
  0.0 63.7 jit_solution(1626797964874721321)
XLA Ops:
  0.6 60.5 %layer.1 = (bf16[8,384]{1,0:T(8,128)(2,1)}, f32[2,8]{1,0:T(2,128)}, bf16[1,3072,128]{2,1,0:T(8,128)(2,1)}, bf16[1,3072,128]{2,1,0:T(8,128)(2,1)}, bf16[1,128,3072]{2,1,0:T(8,128)(2,1)}) custom-call(bf16[8,384]{1,0:T(8,128)(2,1)} %tokens_hbm.1, bf16[8,384]{1,0:T(8,128)(2,1)} %cotangent_hbm.1, bf16[2,8]{1,0:T(2,128)(2,1)} %bitcast.4, s32[2,8]{1,0:T(2,128)} %bitcast.3, ...), custom_call_target="tpu_custom_call" | custom-call | tf_op jit(solution)/shard_map/layer/pallas_call | solution.py:487
  61.2 2.5 %emit.1 = (bf16[8,384]{1,0:T(8,128)(2,1)}, f32[2,8]{1,0:T(2,128)}, bf16[1,3072,128]{2,1,0:T(8,128)(2,1)}, bf16[1,3072,128]{2,1,0:T(8,128)(2,1)}, bf16[1,128,3072]{2,1,0:T(8,128)(2,1)}) custom-call(bf16[8,384]{1,0:T(8,128)(2,1)} %get-tuple-element.15.refs_0_, f32[2,8]{1,0:T(2,128)} %get-tuple-element.16.refs_1_, ...), custom_call_target="tpu_custom_call" | custom-call | tf_op jit(solution)/shard_map/emit/pallas_call | solution.py:571

commit v5 on v4

--- a/solution.py
+++ b/solution.py
@@ -328,28 +328,29 @@
     def columns_of(xi, ci):
         return pl.ds(pl.multiple_of((xi * 2 + ci) * FEAT, 128), FEAT)
 
-    def forward(ci):
-        gate = up = through = None
+    def project(ci, upstream):
+        parts = None
         for xi in range(NX):
             columns = columns_of(xi, ci)
-            terms = (
-                dot(x_ref[:, columns], wg_ref[0, columns, :], 1, 0),
-                dot(x_ref[:, columns], wu_ref[0, columns, :], 1, 0),
-                dot(c_ref[:, columns], wd_ref[0, :, columns], 1, 1),
-            )
-            if gate is None:
-                gate, up, through = terms
+            if upstream:
+                terms = [dot(c_ref[:, columns], wd_ref[0, :, columns], 1, 1)]
             else:
-                gate, up, through = gate + terms[0], up + terms[1], through + terms[2]
-        return gate, up, through
+                terms = [
+                    dot(x_ref[:, columns], wg_ref[0, columns, :], 1, 0),
+                    dot(x_ref[:, columns], wu_ref[0, columns, :], 1, 0),
+                ]
+            parts = terms if parts is None else [a + b for a, b in zip(parts, terms)]
+        return parts
 
     for copy in weights:
         copy.wait()
-    sums[0], sums[1], sums[2] = forward(core)
-    for one in gathers:
-        one.from_sibling()
-    pre_gate, pre_up, hidden_grad = forward(1 - core)
-    pre_gate, pre_up, hidden_grad = pre_gate + sums[0], pre_up + sums[1], hidden_grad + sums[2]
+    sums[0], sums[1] = project(core, False)
+    sums[2] = project(core, True)[0]
+    gathers[0].from_sibling()
+    pre_gate, pre_up = project(1 - core, False)
+    pre_gate, pre_up = pre_gate + sums[0], pre_up + sums[1]
+    gathers[1].from_sibling()
+    hidden_grad = project(1 - core, True)[0] + sums[2]
     sig = jax.nn.sigmoid(pre_gate)
     act = pre_gate * sig
     hidden = act * pre_up

time: 63.9 us -> 64 us (level)
  no operation moved by 1% of the time
where the time goes in v5:
time: 64 us; the launch traced here: 63.8 us
  Pallas kernels  63.2 us (99%)
  between operations  0.64 us (1%)
    pallas_call x1, Pallas kernels, layer(): pl.pallas_call(layer_kernel, name='layer', out_shape=(jax.ShapeDtypeStruc...  60.6 us
    pallas_call x1, Pallas kernels, emit(): pl.pallas_call(emit_kernel, name='emit', out_shape=tuple((jax.ShapeDtypeS...  2.55 us

profile of v5, /device:TPU:2, one launch (start us, length us, event | category | flops | bytes accessed | tf_op | source)
XLA Modules:
  0.0 63.8 jit_solution(3030019889331658762)
XLA Ops:
  0.6 60.6 %layer.1 = (bf16[8,384]{1,0:T(8,128)(2,1)}, f32[2,8]{1,0:T(2,128)}, bf16[1,3072,128]{2,1,0:T(8,128)(2,1)}, bf16[1,3072,128]{2,1,0:T(8,128)(2,1)}, bf16[1,128,3072]{2,1,0:T(8,128)(2,1)}) custom-call(bf16[8,384]{1,0:T(8,128)(2,1)} %tokens_hbm.1, bf16[8,384]{1,0:T(8,128)(2,1)} %cotangent_hbm.1, bf16[2,8]{1,0:T(2,128)(2,1)} %bitcast.4, s32[2,8]{1,0:T(2,128)} %bitcast.3, ...), custom_call_target="tpu_custom_call" | custom-call | tf_op jit(solution)/shard_map/layer/pallas_call | solution.py:488
  61.3 2.5 %emit.1 = (bf16[8,384]{1,0:T(8,128)(2,1)}, f32[2,8]{1,0:T(2,128)}, bf16[1,3072,128]{2,1,0:T(8,128)(2,1)}, bf16[1,3072,128]{2,1,0:T(8,128)(2,1)}, bf16[1,128,3072]{2,1,0:T(8,128)(2,1)}) custom-call(bf16[8,384]{1,0:T(8,128)(2,1)} %get-tuple-element.15.refs_0_, f32[2,8]{1,0:T(2,128)} %get-tuple-element.16.refs_1_, ...), custom_call_target="tpu_custom_call" | custom-call | tf_op jit(solution)/shard_map/emit/pallas_call | solution.py:572
